TPU v7x, 128 devices: a whole 4x4x4 slice. The times are simulated.
128 devices in a mesh: dp: 4 (over x), expert: 32 (over y, z, core).
Axes of the slice: x: 4, y: 4, z: 4, core: 2. Of those that a mesh axis runs over, the one named last changes fastest.
Arguments:
- tokens: bfloat16 [4096, 3584], P(('dp', 'expert')), may hold values from -6 to 6
- expert_ids: int32 [4096, 8], P(('dp', 'expert')), may hold values from 0 to 31, all different within a row; in each aligned block of 32 rows (0 to 31, 32 to 63, ...) at most 12 rows name the same one
- route_weights: float32 [4096, 8], P(('dp', 'expert')), may hold values from 0.1 to 1
- out_grad: bfloat16 [4096, 3584], P(('dp', 'expert')), may hold values from -6 to 6
- gate_weight: bfloat16 [32, 3584, 1024], P('expert', 'dp'), may hold values from -0.09375 to 0.09375
- up_weight: bfloat16 [32, 3584, 1024], P('expert', 'dp'), may hold values from -0.09375 to 0.09375
- down_weight: bfloat16 [32, 1024, 3584], P('expert', None, 'dp'), may hold values from -0.1875 to 0.1875
Outputs:
- mixed: bfloat16 [4096, 3584], P(('dp', 'expert'))
- tokens_grad: bfloat16 [4096, 3584], P(('dp', 'expert'))
- route_grad: float32 [4096, 8], P(('dp', 'expert'))
- gate_grad: bfloat16 [32, 3584, 1024], P('expert', 'dp')
- up_grad: bfloat16 [32, 3584, 1024], P('expert', 'dp')
- down_grad: bfloat16 [32, 1024, 3584], P('expert', None, 'dp')
Inputs may be any that keep to these rules, and one draw needn't show every extreme that they name: `expert_ids`: each row names 8 different experts; in each aligned block of 32 rows (the rows of one device) no expert is named by more than 12 rows, a bound that some block reaches.
All inputs are finite; a program needn't handle non-finite values.
Results may differ from a plain program's by a relative error of at most 0.0065.
Values may be sent and summed in bfloat16 or wider, within the bound.
A program may use at most 192 MiB of HBM per device.

v0:
```python
import jax
import jax.numpy as jnp
from jax import lax
from jax.sharding import PartitionSpec as P


def silu_parts(pre_act):
    sigmoid_val = jax.nn.sigmoid(pre_act)
    return (pre_act * sigmoid_val, sigmoid_val * (1.0 + pre_act * (1.0 - sigmoid_val)))


def route_slots(chosen_ids, experts, slot_most):
    onehot = (chosen_ids[:, :, None] == jnp.arange(experts, dtype=jnp.int32)[None, None, :]).astype(
        jnp.int32
    )
    chosen = jnp.sum(onehot, axis=1)
    before = jnp.cumsum(chosen, axis=0) - chosen
    place = jnp.sum(onehot * before[:, None, :], axis=2)
    return (chosen_ids * slot_most + place, jnp.sum(chosen, axis=0))


def compact_plan(counts_in, slot_most, padded):
    experts = counts_in.shape[0]
    ends = jnp.cumsum(counts_in)
    starts = ends - counts_in
    live_total = ends[-1]
    row_ids = jnp.arange(padded, dtype=jnp.int32)
    source = jnp.minimum(
        jnp.sum((row_ids[:, None] >= ends[None, :]).astype(jnp.int32), axis=1), experts - 1
    )
    source_start = jnp.sum(
        jnp.where(
            jnp.arange(experts, dtype=jnp.int32)[None, :] == source[:, None], starts[None, :], 0
        ),
        axis=1,
    )
    live_rows = row_ids < live_total
    take_rows = jnp.where(live_rows, source * slot_most + row_ids - source_start, 0)
    slot_pos = jnp.arange(slot_most, dtype=jnp.int32)[None, :]
    back_live = slot_pos < counts_in[:, None]
    back_rows = jnp.where(back_live, starts[:, None] + slot_pos, 0)
    return (take_rows, live_rows, back_rows.reshape(-1), back_live.reshape(-1), live_total)


def run_tiles(live_total, tile_fn, buffers):
    tile_count = (live_total + 127) // 128

    def tile_step(tile_index, current):
        tile_start = tile_index * 128
        new_pieces = tile_fn(tile_start)
        return tuple(
            (
                lax.dynamic_update_slice_in_dim(prior_buf, new_piece, tile_start, 0)
                for prior_buf, new_piece in zip(current, new_pieces)
            )
        )

    return lax.fori_loop(0, tile_count, tile_step, buffers)


def contract_rows(first, second):
    return lax.dot_general(
        first, second, (((0,), (0,)), ((), ())), preferred_element_type=jnp.float32
    )


def contract_cols(first, second):
    return lax.dot_general(
        first, second, (((1,), (1,)), ((), ())), preferred_element_type=jnp.float32
    )


def gate_up_terms(hidden_grad, gate_up_rows, hidden_width):
    act_val, act_slope = silu_parts(gate_up_rows[:, :hidden_width])
    up_pre = gate_up_rows[:, hidden_width:]
    return jnp.concatenate(
        [
            (hidden_grad * up_pre * act_slope).astype(jnp.bfloat16),
            (hidden_grad * act_val).astype(jnp.bfloat16),
        ],
        axis=1,
    )


def per_device(tokens, expert_ids, route_weights, out_grad, gate_weight, up_weight, down_weight):
    experts = lax.axis_size("expert")
    tok_rows, model_width = tokens.shape
    choose_k = expert_ids.shape[1]
    hidden_width = gate_weight.shape[2]
    slot_most = min(tok_rows, 3 * tok_rows * choose_k // (2 * experts))
    padded = (experts * slot_most + 127) // 128 * 128
    slot_ids, slot_counts = route_slots(expert_ids, experts, slot_most)
    flat_slots = slot_ids.reshape(-1)
    pick_table = (
        jnp.arange(experts * slot_most, dtype=jnp.int32)[:, None] == flat_slots[None, :]
    ).astype(jnp.bfloat16)
    token_table = jnp.sum(pick_table.reshape(experts * slot_most, tok_rows, choose_k), axis=2)
    outgoing = jnp.dot(token_table, tokens, preferred_element_type=jnp.float32).astype(jnp.bfloat16)
    arrived, arrived_counts = (
        lax.all_to_all(
            outgoing.reshape(experts, slot_most, model_width),
            "expert",
            split_axis=0,
            concat_axis=0,
            tiled=True,
        ),
        lax.all_to_all(
            slot_counts.reshape(experts, 1), "expert", split_axis=0, concat_axis=0, tiled=True
        ),
    )
    take_rows, live_rows, back_rows, back_live, live_total = compact_plan(
        arrived_counts.reshape(-1), slot_most, padded
    )
    zero_bf = jnp.zeros((), jnp.bfloat16)
    compact = jnp.where(
        live_rows[:, None], arrived.reshape(experts * slot_most, model_width)[take_rows], zero_bf
    )
    gate_local = gate_weight[0]
    up_local = up_weight[0]
    down_local = down_weight[0]
    whole_gate, whole_up, whole_down = (
        lax.all_gather(gate_local, "dp", axis=0, tiled=True),
        lax.all_gather(up_local, "dp", axis=0, tiled=True),
        lax.all_gather(down_local, "dp", axis=1, tiled=True),
    )

    def forward_tile(tile_start):
        tile_rows = lax.dynamic_slice_in_dim(compact, tile_start, 128, 0)
        gate_pre = jnp.dot(tile_rows, whole_gate, preferred_element_type=jnp.float32)
        up_pre = jnp.dot(tile_rows, whole_up, preferred_element_type=jnp.float32)
        act_val, unused_slope = silu_parts(gate_pre)
        hidden_tile = (act_val * up_pre).astype(jnp.bfloat16)
        result_tile = jnp.dot(hidden_tile, whole_down, preferred_element_type=jnp.float32).astype(
            jnp.bfloat16
        )
        return (result_tile, jnp.concatenate([gate_pre, up_pre], axis=1), hidden_tile)

    results, gate_up, hidden = run_tiles(
        live_total,
        forward_tile,
        (
            jnp.zeros((padded, model_width), jnp.bfloat16),
            jnp.zeros((padded, 2 * hidden_width), jnp.float32),
            jnp.zeros((padded, hidden_width), jnp.bfloat16),
        ),
    )
    returned = jnp.where(back_live[:, None], results[back_rows], zero_bf).reshape(
        experts, slot_most, model_width
    )
    came_back = lax.all_to_all(returned, "expert", split_axis=0, concat_axis=0, tiled=True)
    per_choice = (
        came_back.reshape(experts * slot_most, model_width)[flat_slots]
        .reshape(tok_rows, choose_k, model_width)
        .astype(jnp.float32)
    )
    mixed = jnp.sum(route_weights[:, :, None] * per_choice, axis=1).astype(jnp.bfloat16)
    grad32 = out_grad.astype(jnp.float32)
    route_grad = jnp.sum(grad32[:, None, :] * per_choice, axis=2)
    out_terms = (
        (route_weights[:, :, None] * grad32[:, None, :])
        .astype(jnp.bfloat16)
        .reshape(tok_rows * choose_k, model_width)
    )
    grad_send = jnp.dot(pick_table, out_terms, preferred_element_type=jnp.float32).astype(
        jnp.bfloat16
    )
    grad_arrived = lax.all_to_all(
        grad_send.reshape(experts, slot_most, model_width),
        "expert",
        split_axis=0,
        concat_axis=0,
        tiled=True,
    )
    grad_compact = jnp.where(
        live_rows[:, None],
        grad_arrived.reshape(experts * slot_most, model_width)[take_rows],
        zero_bf,
    )
    whole_joined = jnp.concatenate([whole_gate, whole_up], axis=1)

    def backward_tile(tile_start):
        grad_tile = lax.dynamic_slice_in_dim(grad_compact, tile_start, 128, 0)
        stored = lax.dynamic_slice_in_dim(gate_up, tile_start, 128, 0)
        hidden_grad = contract_cols(grad_tile, whole_down)
        term_tile = gate_up_terms(hidden_grad, stored, hidden_width)
        input_tile = contract_cols(term_tile, whole_joined).astype(jnp.bfloat16)
        return (term_tile, input_tile)

    gate_up_grad, input_rows = run_tiles(
        live_total,
        backward_tile,
        (
            jnp.zeros((padded, 2 * hidden_width), jnp.bfloat16),
            jnp.zeros((padded, model_width), jnp.bfloat16),
        ),
    )
    pieces, grad_pieces = (
        lax.all_to_all(compact, "dp", split_axis=1, concat_axis=0, tiled=True),
        lax.all_to_all(grad_compact, "dp", split_axis=1, concat_axis=0, tiled=True),
    )
    hidden_all, grads_all = (
        lax.all_gather(hidden, "dp", axis=0, tiled=True),
        lax.all_gather(gate_up_grad, "dp", axis=0, tiled=True),
    )
    joined_grad = contract_rows(pieces, grads_all)
    gate_grad = joined_grad[:, :hidden_width].astype(jnp.bfloat16)[None]
    up_grad = joined_grad[:, hidden_width:].astype(jnp.bfloat16)[None]
    down_grad = contract_rows(hidden_all, grad_pieces).astype(jnp.bfloat16)[None]
    returned_grad = jnp.where(back_live[:, None], input_rows[back_rows], zero_bf).reshape(
        experts, slot_most, model_width
    )
    grad_back = lax.all_to_all(returned_grad, "expert", split_axis=0, concat_axis=0, tiled=True)
    per_choice_grad = grad_back.reshape(experts * slot_most, model_width)[flat_slots].reshape(
        tok_rows, choose_k, model_width
    )
    tokens_grad = jnp.sum(per_choice_grad.astype(jnp.float32), axis=1).astype(jnp.bfloat16)
    return (mixed, tokens_grad, route_grad, gate_grad, up_grad, down_grad)


def solution(mesh):
    return jax.shard_map(
        per_device,
        mesh=mesh,
        in_specs=(
            P(("dp", "expert"), None),
            P(("dp", "expert"), None),
            P(("dp", "expert"), None),
            P(("dp", "expert"), None),
            P("expert", "dp", None),
            P("expert", "dp", None),
            P("expert", None, "dp"),
        ),
        out_specs=(
            P(("dp", "expert"), None),
            P(("dp", "expert"), None),
            P(("dp", "expert"), None),
            P("expert", "dp", None),
            P("expert", "dp", None),
            P("expert", None, "dp"),
        ),
        check_vma=False,
    )
```

profile of v0, /device:TPU:1, one launch (start us, length us, event | category | flops | bytes accessed | tf_op | source)
XLA Modules:
  0.0 562.8 jit_solution(15857799591946311366)
XLA Ops:
  11.1 9.6 %all-to-all-start = ((s32[32,1,1]{2,1,0:T(1,128)}), s32[32,1,1]{2,1,0:T(1,128)S(1)}, u32[]{:S(2)}, u32[]{:S(2)}) async-start(s32[32,1,1]{2,1,0:T(1,128)} %copy.50), calls=%async_computation | async-start | bytes 32768 | tf_op jit(solution)/shard_map/all_to_all | solution.py:107
  36.3 42.1 %all-to-all-done.3 = bf16[32,12,3584]{2,1,0:T(8,128)(2,1)} async-done(((bf16[32,12,3584]{2,1,0:T(8,128)(2,1)}), bf16[32,12,3584]{2,1,0:T(8,128)(2,1)}, u32[]{:S(2)}, u32[]{:S(2)}) %all-to-all-start.3) | async-done | bytes 2752544 | tf_op jit(solution)/shard_map/all_to_all | solution.py:167
  78.4 6.7 %all-to-all-start.1 = ((bf16[32,12,3584]{2,1,0:T(8,128)(2,1)}), bf16[32,12,3584]{2,1,0:T(8,128)(2,1)}, u32[]{:S(2)}, u32[]{:S(2)}) async-start(bf16[32,12,3584]{2,1,0:T(8,128)(2,1)} %reshape.276), calls=%async_computation.1 | async-start | bytes 7340032 | tf_op jit(solution)/shard_map/all_to_all | solution.py:100
  96.4 34.4 %all-to-all-done.1 = bf16[32,12,3584]{2,1,0:T(8,128)(2,1)} async-done(((bf16[32,12,3584]{2,1,0:T(8,128)(2,1)}), bf16[32,12,3584]{2,1,0:T(8,128)(2,1)}, u32[]{:S(2)}, u32[]{:S(2)}) %all-to-all-start.1) | async-done | bytes 2752544 | tf_op jit(solution)/shard_map/all_to_all | solution.py:100
  152.6 23.3 %all-gather.15.cloned.1.call-done = bf16[1,3584,1024]{2,1,0:T(8,128)(2,1)} async-done(((bf16[1,896,1024]{2,1,0:T(8,128)(2,1)}), bf16[1,3584,1024]{2,1,0:T(8,128)(2,1)}) %all-gather.15.cloned.1.call-update) | async-done | bytes 7340048 | tf_op jit(solution)/shard_map/all_gather | solution.py:123
  175.9 13.2 %pad_maximum_fusion.2 = bf16[3584,2048]{1,0:T(8,128)(2,1)} fusion(bf16[3584,1024]{1,0:T(8,128)(2,1)} %bitcast.67, bf16[3584,1024]{1,0:T(8,128)(2,1)} %bitcast.60), kind=kLoop, calls=%fused_computation.30 | loop fusion | flops 29360128 | bytes 29360128 | tf_op jit(solution)/shard_map/concatenate | solution.py:179
  189.1 79.5 %all-gather.17.cloned.1.call-done = bf16[1,1024,3584]{2,1,0:T(8,128)(2,1)} async-done(((bf16[1,1024,896]{2,1,0:T(8,128)(2,1)}), bf16[1,1024,3584]{2,1,0:T(8,128)(2,1)}) %all-gather.17.cloned.1.call-update) | async-done | bytes 7340048 | tf_op jit(solution)/shard_map/all_gather | solution.py:124
  271.8 43.7 %while.26 = (s32[]{:T(128)}, bf16[384,3584]{1,0:T(8,128)(2,1)S(1)}, f32[384,2048]{1,0:T(8,128)}, bf16[384,1024]{1,0:T(8,128)(2,1)}, s32[]{:T(128)}, /*index=5*/b...) while((s32[]{:T(128)}, bf16[384,3584]{1,0:T(8,128)(2,1)S(1)}, ...), condition=%wide.region_9.10_spmd, body=%wide.region_8.9_spmd.sunk | while | flops 2820079616 | bytes 80610560 | solution.py:58
  318.7 55.0 %while.27 = (s32[]{:T(128)}, bf16[384,2048]{1,0:T(8,128)(2,1)}, bf16[384,3584]{1,0:T(8,128)(2,1)}, s32[]{:T(128)}, bf16[384,3584]{1,0:T(8,128)(2,1)}, /*index=5*...) while((s32[]{:T(128)}, bf16[384,2048]{1,0:T(8,128)(2,1)}, ...), condition=%wide.region_12.13_spmd, body=%wide.region_11.12_spmd.sunk | while | flops 2822832128 | bytes 27002560 | solution.py:58
  318.7 6.1 %fusion.59 = (bf16[128,1024]{1,0:T(8,128)(2,1)S(1)}, bf16[128,1024]{1,0:T(8,128)(2,1)S(1)}) fusion(f32[384,2048]{1,0:T(8,128)} %get-tuple-element.363, s32[]{:T(128)S(6)} %select_n.137, s32[]{:T(128)S(6)} %add.143, bf16[1024,3584]{1,0:T(8,128)(2,1)} %get-tuple-element.362, bf16[384,3584]{1,0:T(8,128)(2,1)} %get-tuple-element.361), kind=kOutput, calls=%fused_computation.23.clone.1 | convolution fusion | flops 941228032 | bytes 9831936 | tf_op jit(solution)/shard_map/while/body/dot_general | solution.py:68
  324.8 11.9 %fusion.61 = bf16[384,3584]{1,0:T(8,128)(2,1)} fusion(bf16[384,3584]{1,0:T(8,128)(2,1)} %get-tuple-element.346, s32[]{:T(128)S(6)} %select_n.137, bf16[3584,2048]{1,0:T(8,128)(2,1)} %get-tuple-element.364, bf16[128,1024]{1,0:T(8,128)(2,1)S(1)} %get-tuple-element.290, bf16[128,1024]{1,0:T(8,128)(2,1)S(1)} %get-tuple-element.291), kind=kOutput, calls=%fused_computation.18.clone.1 | convolution fusion | flops 1880555520 | bytes 16121860 | tf_op jit(solution)/shard_map/while/body/dot_general | solution.py:68
  337.5 6.2 %fusion.59 = (bf16[128,1024]{1,0:T(8,128)(2,1)S(1)}, bf16[128,1024]{1,0:T(8,128)(2,1)S(1)}) fusion(f32[384,2048]{1,0:T(8,128)} %get-tuple-element.363, s32[]{:T(128)S(6)} %select_n.137, s32[]{:T(128)S(6)} %add.143, bf16[1024,3584]{1,0:T(8,128)(2,1)} %get-tuple-element.362, bf16[384,3584]{1,0:T(8,128)(2,1)} %get-tuple-element.361), kind=kOutput, calls=%fused_computation.23.clone.1 | convolution fusion | flops 941228032 | bytes 9831936 | tf_op jit(solution)/shard_map/while/body/dot_general | solution.py:68
  343.7 11.2 %fusion.61 = bf16[384,3584]{1,0:T(8,128)(2,1)} fusion(bf16[384,3584]{1,0:T(8,128)(2,1)} %get-tuple-element.346, s32[]{:T(128)S(6)} %select_n.137, bf16[3584,2048]{1,0:T(8,128)(2,1)} %get-tuple-element.364, bf16[128,1024]{1,0:T(8,128)(2,1)S(1)} %get-tuple-element.290, bf16[128,1024]{1,0:T(8,128)(2,1)S(1)} %get-tuple-element.291), kind=kOutput, calls=%fused_computation.18.clone.1 | convolution fusion | flops 1880555520 | bytes 16121860 | tf_op jit(solution)/shard_map/while/body/dot_general | solution.py:68
  355.7 6.1 %fusion.59 = (bf16[128,1024]{1,0:T(8,128)(2,1)S(1)}, bf16[128,1024]{1,0:T(8,128)(2,1)S(1)}) fusion(f32[384,2048]{1,0:T(8,128)} %get-tuple-element.363, s32[]{:T(128)S(6)} %select_n.137, s32[]{:T(128)S(6)} %add.143, bf16[1024,3584]{1,0:T(8,128)(2,1)} %get-tuple-element.362, bf16[384,3584]{1,0:T(8,128)(2,1)} %get-tuple-element.361), kind=kOutput, calls=%fused_computation.23.clone.1 | convolution fusion | flops 941228032 | bytes 9831936 | tf_op jit(solution)/shard_map/while/body/dot_general | solution.py:68
  361.8 11.1 %fusion.61 = bf16[384,3584]{1,0:T(8,128)(2,1)} fusion(bf16[384,3584]{1,0:T(8,128)(2,1)} %get-tuple-element.346, s32[]{:T(128)S(6)} %select_n.137, bf16[3584,2048]{1,0:T(8,128)(2,1)} %get-tuple-element.364, bf16[128,1024]{1,0:T(8,128)(2,1)S(1)} %get-tuple-element.290, bf16[128,1024]{1,0:T(8,128)(2,1)S(1)} %get-tuple-element.291), kind=kOutput, calls=%fused_computation.18.clone.1 | convolution fusion | flops 1880555520 | bytes 16121860 | tf_op jit(solution)/shard_map/while/body/dot_general | solution.py:68
  374.0 9.7 %gather_fusion.4 = bf16[384,3584]{1,0:T(8,128)(2,1)} fusion(bf16[384,3584]{1,0:T(8,128)(2,1)} %get-tuple-element.102, s32[1024]{0:T(1024)S(1)} %pad_clamp_fusion.1), kind=kCustom, calls=%fused_computation.4 | custom fusion | bytes 5506560 | tf_op jit(solution)/shard_map/gather | solution.py:209
  383.7 5.5 gather.32
  393.1 5.3 gather.28
  398.4 5.5 broadcast_select_fusion
  403.9 53.4 %all_to_all.64 = bf16[32,12,3584]{2,1,0:T(8,128)(2,1)} all-to-all(bf16[32,12,3584]{2,1,0:T(8,128)(2,1)} %get-tuple-element.168), channel_id=1, replica_groups=mesh['dp'=4,'expert'=32] {'expert'}, dimensions={0} | all-to-all | bytes 5505024 | tf_op jit(solution)/shard_map/all_to_all | solution.py:212
  457.4 48.8 %all_to_all.65 = bf16[32,12,3584]{2,1,0:T(8,128)(2,1)} all-to-all(bf16[32,12,3584]{2,1,0:T(8,128)(2,1)S(1)} %copy-done.3), channel_id=1, replica_groups=mesh['dp'=4,'expert'=32] {'expert'}, dimensions={0} | all-to-all | bytes 5505024 | tf_op jit(solution)/shard_map/all_to_all | solution.py:150
  531.3 7.4 %convert_bitcast_fusion = bf16[1,1024,896]{2,1,0:T(8,128)(2,1)} fusion(bf16[1536,1024]{1,0:T(8,128)(2,1)} %all-gather.11.cloned.1.call-done, bf16[1536,896]{1,0:T(8,128)(2,1)} %bitcast.16), kind=kOutput, calls=%fused_computation.49 | convolution fusion | flops 2819489792 | bytes 7733248 | tf_op jit(solution)/shard_map/dot_general | solution.py:62
  538.8 5.9 %all-to-all-done.5 = bf16[384,4,896]{2,0,1:T(8,128)(2,1)} async-done(((bf16[384,4,896]{2,0,1:T(8,128)(2,1)}), bf16[384,4,896]{2,0,1:T(8,128)(2,1)}, u32[]{:S(2)}, u32[]{:S(2)}) %all-to-all-start.5) | async-done | bytes 2752544 | tf_op jit(solution)/shard_map/all_to_all | solution.py:198
  544.7 8.9 %convolution_convert_fusion.4 = bf16[896,2048]{1,0:T(8,128)(2,1)S(1)} fusion(bf16[1536,896]{1,0:T(8,128)(2,1)} %bitcast.12, bf16[1536,2048]{1,0:T(8,128)(2,1)} %all-gather.9.cloned.1.call-done), kind=kOutput, calls=%fused_computation.41 | convolution fusion | flops 5638979584 | bytes 12713984 | tf_op jit(solution)/shard_map/dot_general | solution.py:62
  (137 shorter events, 125.2 us)
Async XLA Ops:
  7.2 25.7 %copy-start = (bf16[32,3584]{1,0:T(8,128)(2,1)S(1)}, bf16[32,3584]{1,0:T(8,128)(2,1)}, u32[]{:S(2)}) copy-start(bf16[32,3584]{1,0:T(8,128)(2,1)} %param.11) | copy-start | bytes 688132
  7.2 13.6 %copy-start.10 = (bf16[32,3584]{1,0:T(8,128)(2,1)S(1)}, bf16[32,3584]{1,0:T(8,128)(2,1)}, u32[]{:S(2)}) copy-start(bf16[32,3584]{1,0:T(8,128)(2,1)} %param.14) | copy-start | bytes 688132
  7.2 145.4 %all-gather.13.cloned.1.call-start = ((), (), s32[]{:S(2)}) async-start(), calls=%async_computation.9 | async-start | bytes 9175040 | tf_op jit(solution)/shard_map/all_gather | solution.py:122
  7.9 12.9 %copy-start.14 = (f32[32,8]{0,1:T(8,128)S(1)}, f32[32,8]{0,1:T(8,128)}, u32[]{:S(2)}) copy-start(f32[32,8]{0,1:T(8,128)} %param.13) | copy-start | bytes 3076
  7.9 167.9 %all-gather.15.cloned.1.call-start = ((), (), s32[]{:S(2)}) async-start(), calls=%async_computation.10 | async-start | bytes 9175040 | tf_op jit(solution)/shard_map/all_gather | solution.py:123
  8.7 259.9 %all-gather.17.cloned.1.call-start = ((), (), s32[]{:S(2)}) async-start(), calls=%async_computation.11 | async-start | bytes 9175040 | tf_op jit(solution)/shard_map/all_gather | solution.py:124
  11.1 16.5 %all-to-all-start = ((s32[32,1,1]{2,1,0:T(1,128)}), s32[32,1,1]{2,1,0:T(1,128)S(1)}, u32[]{:S(2)}, u32[]{:S(2)}) async-start(s32[32,1,1]{2,1,0:T(1,128)} %copy.50), calls=%async_computation | async-start | bytes 32768 | tf_op jit(solution)/shard_map/all_to_all | solution.py:107
  20.7 12.0 %copy-start.8 = (s32[32,8]{1,0:T(8,128)}, s32[32,8]{1,0:T(8,128)S(1)}, u32[]{:S(2)}) copy-start(s32[32,8]{1,0:T(8,128)S(1)} %multiply_add_fusion) | copy-start | bytes 3076
  27.6 50.9 %all-to-all-start.3 = ((bf16[32,12,3584]{2,1,0:T(8,128)(2,1)}), bf16[32,12,3584]{2,1,0:T(8,128)(2,1)}, u32[]{:S(2)}, u32[]{:S(2)}) async-start(bf16[32,12,3584]{2,1,0:T(8,128)(2,1)} %reshape.280), calls=%async_computation.3 | async-start | bytes 7340032 | tf_op jit(solution)/shard_map/all_to_all | solution.py:167
  78.4 52.5 %all-to-all-start.1 = ((bf16[32,12,3584]{2,1,0:T(8,128)(2,1)}), bf16[32,12,3584]{2,1,0:T(8,128)(2,1)}, u32[]{:S(2)}, u32[]{:S(2)}) async-start(bf16[32,12,3584]{2,1,0:T(8,128)(2,1)} %reshape.276), calls=%async_computation.1 | async-start | bytes 7340032 | tf_op jit(solution)/shard_map/all_to_all | solution.py:100
  143.1 4.9 copy-start.2
  143.1 260.8 %all-to-all-start.6 = ((bf16[384,4,896]{2,0,1:T(8,128)(2,1)}), bf16[384,4,896]{2,0,1:T(8,128)(2,1)}, u32[]{:S(2)}, u32[]{:S(2)}) async-start(bf16[384,4,896]{2,0,1:T(8,128)(2,1)} %get-tuple-element.172), calls=%async_computation.6 | async-start | bytes 5505024 | tf_op jit(solution)/shard_map/all_to_all | solution.py:199
  148.0 383.3 %all-gather.11.cloned.1.call-start = ((), (), s32[]{:S(2)}) async-start(), calls=%async_computation.8 | async-start | bytes 3932160 | tf_op jit(solution)/shard_map/all_gather | solution.py:202
  282.2 5.4 copy-start.5
  286.9 5.3 slice-start
  293.4 5.4 copy-start.5
  298.0 5.3 slice-start
  304.5 5.4 copy-start.5
  309.1 5.2 slice-start
  315.5 229.1 %all-gather.9.cloned.1.call-start = ((), (), s32[]{:S(2)}) async-start(), calls=%async_computation.7 | async-start | bytes 7864320 | tf_op jit(solution)/shard_map/all_gather | solution.py:203
  403.9 53.4 %copy-start.3 = (bf16[32,12,3584]{2,1,0:T(8,128)(2,1)S(1)}, bf16[32,12,3584]{2,1,0:T(8,128)(2,1)}, u32[]{:S(2)}) copy-start(bf16[32,12,3584]{2,1,0:T(8,128)(2,1)} %get-tuple-element.169) | copy-start | bytes 8257540
  506.2 4.9 copy-start.9
  506.2 38.5 %all-to-all-start.5 = ((bf16[384,4,896]{2,0,1:T(8,128)(2,1)}), bf16[384,4,896]{2,0,1:T(8,128)(2,1)}, u32[]{:S(2)}, u32[]{:S(2)}) async-start(bf16[384,4,896]{2,0,1:T(8,128)(2,1)} %get-tuple-element.173), calls=%async_computation.5 | async-start | bytes 5505024 | tf_op jit(solution)/shard_map/all_to_all | solution.py:198
  544.6 11.2 %copy-start.1 = (bf16[32,3584]{1,0:T(8,128)(2,1)S(1)}, bf16[32,3584]{1,0:T(8,128)(2,1)}, u32[]{:S(2)}) copy-start(bf16[32,3584]{1,0:T(8,128)(2,1)} %param.11) | copy-start | bytes 688132
  (9 other events, 31.3 us)
Sparse Core Ops, SparseCore 0:
  9.7 77.3 all-gather.12
  88.7 87.1 all-gather.14
  177.6 90.9 all-gather.16
  315.7 40.2 all-gather.10
  373.8 66.4 all-gather.8
where the time goes:
time: 571 us; the launch traced here: 563 us
  waiting for transfers between devices  190 us (33%)
  blocking collectives  102 us (18%)
  matrix products  98.2 us (17%)
  local copies, waits for them, and re-layouts  72.5 us (13%)
  other arithmetic  43 us (8%)
  starting transfers between devices  31.4 us (5%)
  between operations  15.2 us (3%)
  loops' own time  10.6 us (2%)
    all_gather x1, waiting for transfers between devices, per_device(): lax.all_gather(down_local, 'dp', axis=1, tiled=True)  79.5 us
    all_to_all x1, blocking collectives, per_device(): lax.all_to_all(returned_grad, 'expert', split_axis=0, concat_axis=0, tile...  53.4 us
    dot_general x6, matrix products, contract_cols(): lax.dot_general(first, second, (((1,), (1,)), ((), ())), preferred_elemen...  52.5 us
    all_to_all x1, blocking collectives, per_device(): lax.all_to_all(returned, 'expert', split_axis=0, concat_axis=0, tiled=True)  48.8 us
    all_to_all x1, waiting for transfers between devices, per_device(): lax.all_to_all(grad_send.reshape(experts, slot_most, model_width), 'exper...  42.1 us
    all_to_all x1, waiting for transfers between devices, per_device(): lax.all_to_all(outgoing.reshape(experts, slot_most, model_width), 'expert...  34.4 us
    all_gather x1, waiting for transfers between devices, per_device(): lax.all_gather(up_local, 'dp', axis=0, tiled=True)  23.3 us
    dot_general x2, matrix products, contract_rows(): lax.dot_general(first, second, (((0,), (0,)), ((), ())), preferred_elemen...  16.4 us
  transfers between devices with their start and end apart: 10, of which 6 were waited for; matrix products, arithmetic and copies ran while one was open for 35% of the time, Pallas kernels for 0%

commit v1 on v0

v1 whole, which is shorter than its diff:
```python
import jax
import jax.numpy as jnp
from jax import lax
from jax.sharding import PartitionSpec as P

BF = jnp.bfloat16
F32 = jnp.float32
LANES = 128


def dot32(a, b, dims):
    return lax.dot_general(a, b, (dims, ((), ())), preferred_element_type=F32)


def route_table(ids, weights, experts):
    onehot = (ids[:, :, None] == jnp.arange(experts, dtype=jnp.int32)).astype(jnp.int32)
    chosen = jnp.sum(onehot, axis=1)
    place = jnp.cumsum(chosen, axis=0) * chosen
    dense = jnp.sum(onehot.astype(F32) * weights[:, :, None], axis=1)
    high = lax.reduce_precision(dense, 8, 7)
    middle = lax.reduce_precision(dense - high, 8, 7)
    low = dense - high - middle
    return jnp.concatenate([place.astype(F32), high, middle, low], axis=1).astype(BF)


def to_slices(array, n_dp):
    rows, width = array.shape
    return lax.all_to_all(array, "dp", split_axis=1, concat_axis=0, tiled=True)


def dispatch(tokens, out_grad, table):
    n_dp = lax.axis_size("dp")
    tok = to_slices(tokens, n_dp)
    grad = to_slices(out_grad, n_dp)
    tab = lax.all_gather(table, "dp", axis=0, tiled=True)
    whole = lax.all_gather(
        jnp.concatenate([tok, grad, tab], axis=1), "expert", axis=0, tiled=False
    )
    return whole, grad, tab


def pick_rows(whole, slots, experts, n_dp, tok_rows, width):
    me = lax.axis_index("expert")
    tab = whole[:, :, 2 * width :].astype(F32)
    lane = jnp.arange(tab.shape[2], dtype=jnp.int32)
    place = jnp.sum(jnp.where(lane == me, tab, 0.0), axis=2)
    weight = jnp.sum(jnp.where((lane >= experts) & (lane % experts == me), tab, 0.0), axis=2)
    rows = n_dp * slots
    row = jnp.arange(rows, dtype=jnp.int32)
    tok = jnp.arange(n_dp * tok_rows, dtype=jnp.int32)
    same = (row[:, None] // slots) == (tok[None, :] // tok_rows)
    hit = same & (place[:, None, :] == (row % slots + 1).astype(F32)[None, :, None])
    picked = lax.dot_general(
        hit.astype(BF), whole[:, :, : 2 * width], (((2,), (1,)), ((0,), (0,))), preferred_element_type=F32
    )
    scale = jnp.sum(jnp.where(hit, weight[:, None, :], 0.0), axis=2)
    x_rows = picked[:, :, :width].astype(BF).reshape(experts * rows, width)
    g_rows = (picked[:, :, width:] * scale[:, :, None]).astype(BF).reshape(experts * rows, width)
    return x_rows, g_rows


def activations(pre, quarter):
    gate, up, hgrad = (pre[:, i * quarter : (i + 1) * quarter].astype(F32) for i in range(3))
    sig = jax.nn.sigmoid(gate)
    act = gate * sig
    slope = sig * (1.0 + gate * (1.0 - sig))
    return jnp.concatenate(
        [(act * up).astype(BF), (hgrad * up * slope).astype(BF), (hgrad * act).astype(BF)], axis=1
    )


def combine(back, ids, grad, tab, slots, experts, n_dp, tok_rows, width):
    tab = tab.astype(F32)
    toks = n_dp * tok_rows
    place = tab[:, :experts]
    weight = tab[:, experts : 2 * experts] + tab[:, 2 * experts : 3 * experts] + tab[:, 3 * experts : 4 * experts]
    row = jnp.arange(n_dp * slots, dtype=jnp.int32)
    tok = jnp.arange(toks, dtype=jnp.int32)
    same = (row[None, :] // slots) == (tok[:, None] // tok_rows)
    hit = same[:, None, :] & (place[:, :, None] == (row % slots + 1).astype(F32))
    flat = hit.reshape(toks, -1)
    scaled = jnp.where(hit, weight[:, :, None], 0.0).reshape(toks, -1)
    out_rows = back[:, :width]
    in_rows = back[:, width:]
    mixed = lax.dot_general(
        scaled, out_rows.astype(F32), (((1,), (0,)), ((), ())), precision=lax.Precision.HIGHEST
    )
    tgrad = dot32(flat.astype(BF), in_rows, ((1,), (0,)))
    dots = dot32(grad, out_rows, ((1,), (1,)))
    route = jnp.sum(jnp.where(hit, dots.reshape(hit.shape), 0.0), axis=2)
    mixed = lax.all_to_all(mixed.astype(BF).reshape(n_dp, tok_rows, width), "dp", 0, 0, tiled=True)
    tgrad = lax.all_to_all(tgrad.astype(BF).reshape(n_dp, tok_rows, width), "dp", 0, 0, tiled=True)
    route = lax.psum_scatter(route, "dp", scatter_dimension=0, tiled=True)
    mixed = mixed.transpose(1, 0, 2).reshape(tok_rows, n_dp * width)
    tgrad = tgrad.transpose(1, 0, 2).reshape(tok_rows, n_dp * width)
    onehot = ids[:, :, None] == jnp.arange(experts, dtype=jnp.int32)
    route = jnp.sum(jnp.where(onehot, route[:, None, :], 0.0), axis=2)
    return mixed, tgrad, route


def per_device(tokens, ids, weights, out_grad, gate_weight, up_weight, down_weight):
    experts = lax.axis_size("expert")
    n_dp = lax.axis_size("dp")
    tok_rows, model = tokens.shape
    width = model // n_dp
    hidden = gate_weight.shape[2]
    quarter = hidden // n_dp
    slots = min(tok_rows, 3 * tok_rows * ids.shape[1] // (2 * experts))
    gate, up, down = gate_weight[0], up_weight[0], down_weight[0]

    table = route_table(ids, weights, experts)
    whole, grad, tab = dispatch(tokens, out_grad, table)
    x_rows, g_rows = pick_rows(whole, slots, experts, n_dp, tok_rows, width)

    rows = x_rows.shape[0]
    part = jnp.stack(
        [
            dot32(x_rows, gate, ((1,), (0,))).astype(BF),
            dot32(x_rows, up, ((1,), (0,))).astype(BF),
            dot32(g_rows, down, ((1,), (1,))).astype(BF),
        ]
    )
    part = part.reshape(3, rows, n_dp, quarter).transpose(2, 1, 0, 3).reshape(n_dp * rows, 3 * quarter)
    pre = lax.psum_scatter(part, "dp", scatter_dimension=0, tiled=True)
    acts = activations(pre, quarter)
    terms = lax.all_gather(acts, "dp", axis=0, tiled=False)
    terms = terms.reshape(n_dp, rows, 3, quarter).transpose(2, 1, 0, 3).reshape(3, rows, hidden)
    hid, gterm, uterm = terms[0], terms[1], terms[2]

    out_rows = dot32(hid, down, ((1,), (0,))).astype(BF)
    in_rows = (dot32(gterm, gate, ((1,), (1,))) + dot32(uterm, up, ((1,), (1,)))).astype(BF)
    send = jnp.concatenate([out_rows, in_rows], axis=1).reshape(experts, n_dp * slots, 2 * width)
    back = lax.all_to_all(send, "expert", split_axis=0, concat_axis=0, tiled=True)
    back = back.reshape(experts * n_dp * slots, 2 * width)

    gate_grad = dot32(x_rows, gterm, ((0,), (0,))).astype(BF)[None]
    up_grad = dot32(x_rows, uterm, ((0,), (0,))).astype(BF)[None]
    down_grad = dot32(hid, g_rows, ((0,), (0,))).astype(BF)[None]

    mixed, tgrad, route = combine(back, ids, grad, tab, slots, experts, n_dp, tok_rows, width)
    return (mixed, tgrad, route, gate_grad, up_grad, down_grad)


def solution(mesh):
    rows = P(("dp", "expert"), None)
    weights = (P("expert", "dp", None), P("expert", "dp", None), P("expert", None, "dp"))
    return jax.shard_map(
        per_device,
        mesh=mesh,
        in_specs=(rows, rows, rows, rows) + weights,
        out_specs=(rows, rows, rows) + weights,
        check_vma=False,
    )
```

time: 571 us -> 521 us (0.912)
  the two profiles are of different devices: /device:TPU:1 before, /device:TPU:34 now
where the time goes in v1:
time: 521 us; the launch traced here: 510 us
  waiting for transfers between devices  317 us (61%)
  local copies, waits for them, and re-layouts  62 us (12%)
  matrix products  56.3 us (11%)
  starting transfers between devices  26.7 us (5%)
  other arithmetic  22.1 us (4%)
  between operations  14.6 us (3%)
  blocking collectives  11.9 us (2%)
    all_gather x1, waiting for transfers between devices, per_device(): terms = lax.all_gather(acts, 'dp', axis=0, tiled=False)  93 us
    reduce_scatter x1, waiting for transfers between devices, per_device(): pre = lax.psum_scatter(part, 'dp', scatter_dimension=0, tiled=True)  87.8 us
    all_gather x1, waiting for transfers between devices, dispatch(): lax.all_gather(jnp.concatenate([tok, grad, tab], axis=1), 'expert', axis=...  71.4 us
    all_to_all x1, waiting for transfers between devices, per_device(): lax.all_to_all(send, 'expert', split_axis=0, concat_axis=0, tiled=True)  61.8 us
    dot_general x11, matrix products, dot32(): return lax.dot_general(a, b, (dims, ((), ())), preferred_element_type=F32)  45.9 us
    unnamed x31, local copies, waits for them, and re-layouts  18.1 us
    reshape x1, local copies, waits for them, and re-layouts, per_device(): terms.reshape(n_dp, rows, 3, quarter).transpose(2, 1, 0, 3)  15.5 us
    all_gather x1, blocking collectives, dispatch(): tab = lax.all_gather(table, 'dp', axis=0, tiled=True)  11.9 us
  transfers between devices with their start and end apart: 9, of which 6 were waited for; matrix products, arithmetic and copies ran while one was open for 6% of the time, Pallas kernels for 0%

profile of v1, /device:TPU:34, one launch (start us, length us, event | category | flops | bytes accessed | tf_op | source)
XLA Modules:
  0.0 510.5 jit_solution(16522338820058106155)
XLA Ops:
  9.0 4.8 all-to-all-start.1
  18.8 4.8 all-to-all-start
  23.7 11.9 %all_gather.15 = bf16[128,128]{1,0:T(8,128)(2,1)S(1)} all-gather(bf16[32,128]{1,0:T(8,128)(2,1)S(1)} %pad_maximum_fusion.4), channel_id=1, replica_groups=mesh['dp'=4,'expert'=32] {'dp'}, dimensions={0}, use_global_device_ids=true | all-gather | bytes 40960 | tf_op jit(solution)/shard_map/all_gather | solution.py:35
  36.7 71.4 %all-gather.5.cloned.1.call-done = bf16[4096,1920]{1,0:T(8,128)(2,1)} async-done(((bf16[128,1920]{1,0:T(8,128)(2,1)}), bf16[4096,1920]{1,0:T(8,128)(2,1)}) %all-gather.5.cloned.1.call-update) | async-done | bytes 15728656 | tf_op jit(solution)/shard_map/all_gather | solution.py:36
  110.1 6.4 %fusion = f32[32,48,1792]{2,1,0:T(8,128)S(1)} fusion(bf16[32,128,1920]{2,1,0:T(8,128)(2,1)} %bitcast.95, f32[32,128]{1,0:T(8,128)S(1)} %get-tuple-element.13, f32[48]{0:T(128)S(1)} %fusion.41, pred[48,128]{1,0:T(8,128)(4,1)S(1)} %broadcast_compare_fusion), kind=kOutput, calls=%fused_computation | convolution fusion | flops 705036288 | bytes 25712832 | tf_op jit(solution)/shard_map/dot_general | solution.py:53
  120.0 3.7 convolution_convert_fusion
  126.2 3.8 convolution_convert_fusion.2
  132.5 4.0 convolution_convert_fusion.1
  138.9 9.2 %pad_maximum_fusion = bf16[3,1536,4,256]{1,2,3,0:T(4,128)(2,1)} fusion(bf16[1,1536,4,256]{1,2,3,0:T(4,128)(2,1)S(1)} %copy.90, bf16[1,1536,4,256]{1,2,3,0:T(4,128)(2,1)S(1)} %copy.89, bf16[1,1536,4,256]{1,2,3,0:T(4,128)(2,1)S(1)} %copy.88), kind=kLoop, calls=%fused_computation.2 | loop fusion | flops 9437184 | bytes 18874368 | tf_op jit(solution)/shard_map/stack | solution.py:116
  148.1 10.3 %copy.105 = bf16[96,8,4,1536]{3,1,2,0:T(8,128)(2,1)} copy(bf16[96,8,4,1536]{3,2,1,0:T(4,128)(2,1)} %bitcast.98) | data formatting | bytes 18874368
  158.6 87.8 %reduce-scatter.5.cloned.1.call-done = bf16[1536,768]{0,1:T(8,128)(2,1)} async-done(((bf16[6144,768]{0,1:T(8,128)(2,1)}), bf16[1536,768]{0,1:T(8,128)(2,1)}) %reduce-scatter.5.cloned.1.call-update) | async-done | bytes 2359312 | tf_op jit(solution)/shard_map/reduce_scatter | solution.py:124
  250.5 93.0 %all-gather.7.cloned.1.call-done = bf16[6144,768]{0,1:T(8,128)(2,1)} async-done(((bf16[1536,768]{0,1:T(8,128)(2,1)}), bf16[6144,768]{0,1:T(8,128)(2,1)}) %all-gather.7.cloned.1.call-update) | async-done | bytes 9437200 | tf_op jit(solution)/shard_map/all_gather | solution.py:126
  343.5 15.5 %reshape.277 = bf16[4,1536,3,256]{1,0,3,2:T(4,128)(2,1)} reshape(bf16[6144,768]{0,1:T(8,128)(2,1)} %all-gather.7.cloned.1.call-done) | data formatting | bytes 18874368 | tf_op jit(solution)/shard_map/reshape | solution.py:127
  359.0 6.0 %fusion.42 = (bf16[1,1536,4,256]{1,2,3,0:T(4,128)(2,1)S(1)}, bf16[1,1536,4,256]{1,2,3,0:T(4,128)(2,1)S(1)}, bf16[1,1536,4,256]{1,2,3,0:T(4,128)(2,1)S(1)}) fusion(bf16[3,1536,4,256]{1,2,3,0:T(4,128)(2,1)} %bitcast.97), kind=kLoop, calls=%fused_computation.93 | loop fusion | bytes 18874368 | tf_op jit(solution)/shard_map/slice | solution.py:128
  372.1 3.3 convolution_convert_fusion.3
  381.5 8.1 %copy.94 = bf16[1536,1792]{1,0:T(8,128)(2,1)} copy(bf16[1536,1792]{0,1:T(8,128)(2,1)} %pad_maximum_fusion.1) | data formatting | bytes 11010048 | tf_op jit(solution)/shard_map/concatenate | solution.py:132
  389.6 7.6 %all-to-all-start.2 = ((bf16[32,48,1792]{2,1,0:T(8,128)(2,1)}), bf16[32,48,1792]{2,1,0:T(8,128)(2,1)}, u32[]{:S(2)}, u32[]{:S(2)}) async-start(bf16[32,48,1792]{2,1,0:T(8,128)(2,1)} %bitcast.99), calls=%async_computation.3 | async-start | bytes 11010048 | tf_op jit(solution)/shard_map/all_to_all | solution.py:133
  398.3 7.5 %convert_bitcast_fusion = bf16[1,1024,896]{2,1,0:T(8,128)(2,1)} fusion(bf16[1536,1024]{0,1:T(8,128)(2,1)} %bitcast.105, bf16[1536,896]{1,0:T(8,128)(2,1)} %bitcast.114), kind=kOutput, calls=%fused_computation.36 | convolution fusion | flops 2819489792 | bytes 7733248 | tf_op jit(solution)/shard_map/dot_general | solution.py:12
  405.8 4.4 convert_bitcast_fusion.1
  410.2 61.8 %all-to-all-done.2 = bf16[32,48,1792]{2,1,0:T(8,128)(2,1)} async-done(((bf16[32,48,1792]{2,1,0:T(8,128)(2,1)}), bf16[32,48,1792]{2,1,0:T(8,128)(2,1)}, u32[]{:S(2)}, u32[]{:S(2)}) %all-to-all-start.2) | async-done | bytes 5505056 | tf_op jit(solution)/shard_map/all_to_all | solution.py:133
  478.9 4.5 all-to-all-start.4
  483.4 4.0 fusion.27
  488.5 4.9 all-to-all-start.3
  493.4 7.1 %convert_bitcast_fusion.2 = bf16[1,896,1024]{2,1,0:T(8,128)(2,1)} fusion(bf16[1536,896]{1,0:T(8,128)(2,1)} %bitcast.111, bf16[1536,1024]{0,1:T(8,128)(2,1)} %bitcast.101), kind=kOutput, calls=%fused_computation.38 | convolution fusion | flops 2819489792 | bytes 7733248 | tf_op jit(solution)/shard_map/dot_general | solution.py:12
  (88 shorter events, 49.9 us)
Async XLA Ops:
  7.2 119.0 %copy-start = (bf16[1,896,1024]{2,1,0:T(8,128)(2,1)S(1)}, bf16[1,896,1024]{2,1,0:T(8,128)(2,1)}, u32[]{:S(2)}) copy-start(bf16[1,896,1024]{2,1,0:T(8,128)(2,1)} %param.11) | copy-start | bytes 5505028
  9.0 9.9 %all-to-all-start.1 = ((bf16[32,4,896]{2,0,1:T(8,128)(2,1)}), bf16[32,4,896]{2,0,1:T(8,128)(2,1)S(1)}, u32[]{:S(2)}, u32[]{:S(2)}) async-start(bf16[32,4,896]{2,0,1:T(8,128)(2,1)} %bitcast.92), calls=%async_computation.1 | async-start | bytes 458752 | tf_op jit(solution)/shard_map/all_to_all | solution.py:28
  18.8 16.8 %all-to-all-start = ((bf16[32,4,896]{2,0,1:T(8,128)(2,1)}), bf16[32,4,896]{2,0,1:T(8,128)(2,1)S(1)}, u32[]{:S(2)}, u32[]{:S(2)}) async-start(bf16[32,4,896]{2,0,1:T(8,128)(2,1)} %bitcast.93), calls=%async_computation | async-start | bytes 458752 | tf_op jit(solution)/shard_map/all_to_all | solution.py:28
  23.6 84.5 %all-gather.5.cloned.1.call-start = ((), (), s32[]{:S(2)}) async-start(), calls=%async_computation.8 | async-start | bytes 16220160 | tf_op jit(solution)/shard_map/all_gather | solution.py:36
  36.5 209.9 %reduce-scatter.5.cloned.1.call-start = ((), (), s32[]{:S(2)}) async-start(), calls=%async_computation.7 | async-start | bytes 11796480 | tf_op jit(solution)/shard_map/reduce_scatter | solution.py:124
  117.2 15.3 %copy-start.6 = (bf16[32,48,896]{2,1,0:T(8,128)(2,1)}, bf16[32,48,896]{2,1,0:T(8,128)(2,1)S(1)}, u32[]{:S(2)}) copy-start(bf16[32,48,896]{2,1,0:T(8,128)(2,1)S(1)} %slice.117) | copy-start | bytes 8257540
  117.2 2.9 copy-start.9
  117.6 6.2 %copy-start.8 = (bf16[32,48,896]{2,1,0:T(8,128)(2,1)}, bf16[32,48,896]{2,1,0:T(8,128)(2,1)S(1)}, u32[]{:S(2)}) copy-start(bf16[32,48,896]{2,1,0:T(8,128)(2,1)S(1)} %fusion.2) | copy-start | bytes 8257540
  130.0 2.5 copy-start.11
  158.5 185.0 %all-gather.7.cloned.1.call-start = ((), (), s32[]{:S(2)}) async-start(), calls=%async_computation.9 | async-start | bytes 11796480 | tf_op jit(solution)/shard_map/all_gather | solution.py:126
  365.6 3.0 copy-start.2
  369.2 6.2 %copy-start.3 = (bf16[1,1536,4,256]{1,3,2,0:T(8,128)(2,1)}, bf16[1,1536,4,256]{1,3,2,0:T(8,128)(2,1)S(1)}, u32[]{:S(2)}) copy-start(bf16[1,1536,4,256]{1,3,2,0:T(8,128)(2,1)S(1)} %copy.93) | copy-start | bytes 9437188
  369.2 2.9 copy-start.10
  369.8 5.6 %copy-start.5 = (bf16[1,1536,4,256]{1,3,2,0:T(8,128)(2,1)}, bf16[1,1536,4,256]{1,3,2,0:T(8,128)(2,1)S(1)}, u32[]{:S(2)}) copy-start(bf16[1,1536,4,256]{1,3,2,0:T(8,128)(2,1)S(1)} %copy.91) | copy-start | bytes 9437188
  372.1 3.4 copy-start.12
  389.6 82.5 %all-to-all-start.2 = ((bf16[32,48,1792]{2,1,0:T(8,128)(2,1)}), bf16[32,48,1792]{2,1,0:T(8,128)(2,1)}, u32[]{:S(2)}, u32[]{:S(2)}) async-start(bf16[32,48,1792]{2,1,0:T(8,128)(2,1)} %bitcast.99), calls=%async_computation.3 | async-start | bytes 11010048 | tf_op jit(solution)/shard_map/all_to_all | solution.py:133
  397.2 103.3 %reduce-scatter.7.cloned.1.call-start = ((), (), s32[]{:S(2)}) async-start(), calls=%async_computation.10 | async-start | bytes 81920 | tf_op jit(solution)/shard_map/reduce_scatter | solution.py:93
  398.2 7.5 %copy-start.4 = (bf16[1,1536,4,256]{1,3,2,0:T(8,128)(2,1)S(1)}, bf16[1,1536,4,256]{1,3,2,0:T(8,128)(2,1)}, u32[]{:S(2)}) copy-start(bf16[1,1536,4,256]{1,3,2,0:T(8,128)(2,1)} %copy-done.3) | copy-start | bytes 9437188
  398.3 7.5 %copy-start.7 = (bf16[32,48,896]{2,1,0:T(8,128)(2,1)S(1)}, bf16[32,48,896]{2,1,0:T(8,128)(2,1)}, u32[]{:S(2)}) copy-start(bf16[32,48,896]{2,1,0:T(8,128)(2,1)} %copy-done.6) | copy-start | bytes 8257540
  478.9 9.7 %all-to-all-start.4 = ((bf16[4,32,896]{2,1,0:T(8,128)(2,1)}), bf16[4,32,896]{2,1,0:T(8,128)(2,1)S(1)}, u32[]{:S(2)}, u32[]{:S(2)}) async-start(bf16[4,32,896]{2,1,0:T(8,128)(2,1)} %bitcast.25), calls=%async_computation.5 | async-start | bytes 458752 | tf_op jit(solution)/shard_map/all_to_all | solution.py:92
  488.5 14.3 %all-to-all-start.3 = ((bf16[4,32,896]{2,1,0:T(8,128)(2,1)}), bf16[4,32,896]{2,1,0:T(8,128)(2,1)S(1)}, u32[]{:S(2)}, u32[]{:S(2)}) async-start(bf16[4,32,896]{2,1,0:T(8,128)(2,1)} %bitcast.23), calls=%async_computation.4 | async-start | bytes 458752 | tf_op jit(solution)/shard_map/all_to_all | solution.py:91
  493.4 10.1 %copy-start.1 = (bf16[1,896,1024]{2,1,0:T(8,128)(2,1)S(1)}, bf16[1,896,1024]{2,1,0:T(8,128)(2,1)}, u32[]{:S(2)}) copy-start(bf16[1,896,1024]{2,1,0:T(8,128)(2,1)} %param.11) | copy-start | bytes 5505028
Sparse Core Ops, SparseCore 0:
  36.6 71.4 all-gather.4
  158.6 87.6 reduce-scatter.4
  250.6 92.8 all-gather.6
  475.9 15.6 reduce-scatter.6

commit v2 on v1

--- a/solution.py
+++ b/solution.py
@@ -1,6 +1,10 @@
+import functools
+
 import jax
 import jax.numpy as jnp
 from jax import lax
+from jax.experimental import pallas as pl
+from jax.experimental.pallas import tpu as pltpu
 from jax.sharding import PartitionSpec as P
 
 BF = jnp.bfloat16
@@ -57,16 +61,6 @@
     x_rows = picked[:, :, :width].astype(BF).reshape(experts * rows, width)
     g_rows = (picked[:, :, width:] * scale[:, :, None]).astype(BF).reshape(experts * rows, width)
     return x_rows, g_rows
-
-
-def activations(pre, quarter):
-    gate, up, hgrad = (pre[:, i * quarter : (i + 1) * quarter].astype(F32) for i in range(3))
-    sig = jax.nn.sigmoid(gate)
-    act = gate * sig
-    slope = sig * (1.0 + gate * (1.0 - sig))
-    return jnp.concatenate(
-        [(act * up).astype(BF), (hgrad * up * slope).astype(BF), (hgrad * act).astype(BF)], axis=1
-    )
 
 
 def combine(back, ids, grad, tab, slots, experts, n_dp, tok_rows, width):
@@ -98,13 +92,274 @@
     return mixed, tgrad, route
 
 
+CHUNKS = 4
+MESH = pl.DeviceIdType.MESH
+
+
+def exchange_kernel(
+    slots_dp, x_ref, g_ref, gate_ref, up_ref, down_ref, back_ref, terms_ref,
+    part, own, in_half, in_full, terms, rows_out,
+    ring_send, ring_recv, ret_send, ret_recv, out_sem,
+):
+    n_dp = lax.axis_size("dp")
+    experts = lax.axis_size("expert")
+    d = lax.axis_index("dp")
+    e = lax.axis_index("expert")
+    group = experts // CHUNKS
+    chunk = group * slots_dp
+    half = chunk // 2
+    quarter = own.shape[3]
+    width = x_ref.shape[1]
+    to = ((d + n_dp - 1) % n_dp, (d + 1) % n_dp)
+
+    barrier = pltpu.get_barrier_semaphore()
+    for side in to:
+        pl.semaphore_signal(barrier, inc=1, device_id={"dp": side}, device_id_type=MESH)
+
+    def greet(step, carry):
+        pl.semaphore_signal(
+            barrier, inc=1, device_id={"expert": (e + step) % experts}, device_id_type=MESH
+        )
+        return carry
+
+    lax.fori_loop(1, experts, greet, 0)
+    pl.semaphore_wait(barrier, experts + 1)
+
+    def which(k):
+        return (e // group + k) % CHUNKS
+
+    def rows_of(k, part_half=None):
+        start = which(k) * chunk
+        if part_half is None:
+            return pl.ds(pl.multiple_of(start, chunk), chunk)
+        return pl.ds(pl.multiple_of(start + part_half * half, half), half)
+
+    def cols_of(q):
+        return pl.ds(pl.multiple_of(q * quarter, quarter), quarter)
+
+    def copy(k, way, number, source, target):
+        return pltpu.make_async_remote_copy(
+            src_ref=source,
+            dst_ref=target,
+            send_sem=ring_send.at[k, way, number],
+            recv_sem=ring_recv.at[k, way, number],
+            device_id={"dp": to[way]},
+            device_id_type=MESH,
+        )
+
+    def toward(k, way):
+        return part.at[k, 2 if way == 0 else 0]
+
+    def halves(ref, h):
+        return ref.at[:, pl.ds(h * half, half), :]
+
+    def rs_copy(k, way, number):
+        if number == 0:
+            return copy(k, way, 0, halves(part.at[k, 1], way), in_half.at[k, way])
+        h = way if number == 2 else 1 - way
+        return copy(k, way, number, halves(toward(k, way), h), halves(in_full.at[k, way], h))
+
+    def ag_copy(k, way, number):
+        if number == 5:
+            q = (d + 1) % n_dp if way == 0 else (d + n_dp - 1) % n_dp
+            h = way
+        else:
+            q = d
+            h = way if number == 3 else 1 - way
+        ref = terms.at[:, rows_of(k, h), cols_of(q)]
+        return copy(k, way, number, ref, ref)
+
+    def ag_arrival(k, way, number):
+        src = (d + 1) % n_dp if way == 0 else (d + n_dp - 1) % n_dp
+        q = (d + 2) % n_dp if number == 5 else src
+        h = way if number in (3, 5) else 1 - way
+        ref = terms.at[:, rows_of(k, h), cols_of(q)]
+        return copy(k, way, number, ref, ref)
+
+    def partial(k, q, i):
+        if i == 0:
+            return jnp.dot(x_ref[rows_of(k), :], gate_ref[:, cols_of(q)], preferred_element_type=F32)
+        if i == 1:
+            return jnp.dot(x_ref[rows_of(k), :], up_ref[:, cols_of(q)], preferred_element_type=F32)
+        return dot32(g_ref[rows_of(k), :], down_ref[cols_of(q), :], ((1,), (1,)))
+
+    def stage0(k):
+        def one(step, carry):
+            m = (step + 1) % (n_dp - 1)
+            q = (d + m + 1) % n_dp
+            for i in range(3):
+                part[k, m, i] = partial(k, q, i).astype(BF)
+            return carry
+
+        lax.fori_loop(0, n_dp - 1, one, 0)
+        for way in range(2):
+            rs_copy(k, way, 0).start()
+        for way in range(2):
+            rs_copy(k, way, 1).start()
+        for i in range(3):
+            own[k, i] = partial(k, d, i)
+
+    def stage1(k):
+        for way in range(2):
+            rs_copy(k, way, 0).wait_recv()
+            m = 2 if way == 0 else 0
+            for i in range(3):
+                span = pl.ds(way * half, half)
+                total = part[k, m, i, span, :].astype(F32) + in_half[k, way, i].astype(F32)
+                part[k, m, i, span, :] = total.astype(BF)
+            rs_copy(k, way, 2).start()
+
+    def stage2(k):
+        for number in (1, 2):
+            for way in range(2):
+                rs_copy(k, way, number).wait_recv()
+
+        def total(i, span):
+            return own[k, i, span, :] + in_full[k, 0, i, span, :].astype(F32) + in_full[k, 1, i, span, :].astype(F32)
+
+        step_rows = half // 2
+
+        def act(step, carry):
+            span = pl.ds(pl.multiple_of(step * step_rows, step_rows), step_rows)
+            gate = total(0, span)
+            up = total(1, span)
+            hgrad = total(2, span)
+            sig = jax.nn.sigmoid(gate)
+            val = gate * sig
+            slope = sig * (1.0 + gate * (1.0 - sig))
+            target = pl.ds(pl.multiple_of(which(k) * chunk + step * step_rows, step_rows), step_rows)
+            terms[0, target, cols_of(d)] = (val * up).astype(BF)
+            terms[1, target, cols_of(d)] = (hgrad * up * slope).astype(BF)
+            terms[2, target, cols_of(d)] = (hgrad * val).astype(BF)
+            return carry
+
+        lax.fori_loop(0, chunk // step_rows, act, 0)
+        for number in (3, 4):
+            for way in range(2):
+                ag_copy(k, way, number).start()
+
+    def stage3(k):
+        for way in range(2):
+            ag_arrival(k, way, 3).wait_recv()
+            ag_copy(k, way, 5).start()
+
+    def back_copy(k, i):
+        j = which(k) * group + (e + i) % group
+        return pltpu.make_async_remote_copy(
+            src_ref=rows_out.at[pl.ds(pl.multiple_of(j * slots_dp, slots_dp), slots_dp), :],
+            dst_ref=back_ref.at[pl.ds(pl.multiple_of(e * slots_dp, slots_dp), slots_dp), :],
+            send_sem=ret_send.at[j],
+            recv_sem=ret_recv.at[e],
+            device_id={"expert": j},
+            device_id_type=MESH,
+        )
+
+    def self_copy():
+        mine = pl.ds(pl.multiple_of(e * slots_dp, slots_dp), slots_dp)
+        return pltpu.make_async_copy(rows_out.at[mine, :], back_ref.at[mine, :], out_sem.at[CHUNKS])
+
+    def terms_copy(k):
+        return pltpu.make_async_copy(
+            terms.at[:, rows_of(k), :], terms_ref.at[:, rows_of(k), :], out_sem.at[k]
+        )
+
+    def stage4(k):
+        for way in range(2):
+            ag_arrival(k, way, 4).wait_recv()
+        for way in range(2):
+            ag_arrival(k, way, 5).wait_recv()
+        terms_copy(k).start()
+
+        def one(h, carry):
+            span = pl.ds(pl.multiple_of(which(k) * chunk + h * half, half), half)
+            rows_out[span, :width] = jnp.dot(
+                terms[0, span, :], down_ref[...], preferred_element_type=F32
+            ).astype(BF)
+            rows_out[span, width:] = (
+                dot32(terms[1, span, :], gate_ref[...], ((1,), (1,)))
+                + dot32(terms[2, span, :], up_ref[...], ((1,), (1,)))
+            ).astype(BF)
+            return carry
+
+        lax.fori_loop(0, 2, one, 0)
+        if k == 0:
+            self_copy().start()
+
+        def send(i, carry):
+            back_copy(k, i).start()
+            return carry
+
+        lax.fori_loop(1 if k == 0 else 0, group, send, 0)
+
+    for t in range(CHUNKS + 4):
+        for lag, stage in ((1, stage1), (2, stage2), (3, stage3), (0, stage0), (4, stage4)):
+            if 0 <= t - lag < CHUNKS:
+                stage(t - lag)
+
+    for k in range(CHUNKS):
+        for way in range(2):
+            for number in range(3):
+                rs_copy(k, way, number).wait_send()
+                ag_copy(k, way, number + 3).wait_send()
+        terms_copy(k).wait()
+
+        def sent(i, carry):
+            back_copy(k, i).wait_send()
+            return carry
+
+        lax.fori_loop(1 if k == 0 else 0, group, sent, 0)
+    self_copy().wait()
+
+    def arrived(step, carry):
+        s = (e + step) % experts
+        ref = back_ref.at[pl.ds(pl.multiple_of(s * slots_dp, slots_dp), slots_dp), :]
+        pltpu.make_async_remote_copy(
+            src_ref=ref, dst_ref=ref, send_sem=ret_send.at[s], recv_sem=ret_recv.at[s],
+            device_id={"expert": s}, device_id_type=MESH,
+        ).wait_recv()
+        return carry
+
+    lax.fori_loop(1, experts, arrived, 0)
+
+
+def exchange(x_rows, g_rows, gate, up, down, experts, n_dp):
+    rows, width = x_rows.shape
+    hidden = gate.shape[1]
+    quarter = hidden // n_dp
+    chunk = rows // CHUNKS
+    dma = pltpu.SemaphoreType.DMA
+    return pl.pallas_call(
+        functools.partial(exchange_kernel, rows // experts),
+        out_shape=(
+            jax.ShapeDtypeStruct((rows, 2 * width), BF),
+            jax.ShapeDtypeStruct((3, rows, hidden), BF),
+        ),
+        in_specs=[pl.BlockSpec(memory_space=pltpu.VMEM)] * 5,
+        out_specs=(pl.BlockSpec(memory_space=pl.ANY), pl.BlockSpec(memory_space=pl.ANY)),
+        scratch_shapes=[
+            pltpu.VMEM((CHUNKS, n_dp - 1, 3, chunk, quarter), BF),
+            pltpu.VMEM((CHUNKS, 3, chunk, quarter), F32),
+            pltpu.VMEM((CHUNKS, 2, 3, chunk // 2, quarter), BF),
+            pltpu.VMEM((CHUNKS, 2, 3, chunk, quarter), BF),
+            pltpu.VMEM((3, rows, hidden), BF),
+            pltpu.VMEM((rows, 2 * width), BF),
+            dma((CHUNKS, 2, 6)),
+            dma((CHUNKS, 2, 6)),
+            dma((experts,)),
+            dma((experts,)),
+            dma((CHUNKS + 1,)),
+        ],
+        compiler_params=pltpu.CompilerParams(
+            collective_id=0, has_side_effects=True, vmem_limit_bytes=63 * 1024 * 1024
+        ),
+    )(x_rows, g_rows, gate, up, down)
+
+
 def per_device(tokens, ids, weights, out_grad, gate_weight, up_weight, down_weight):
     experts = lax.axis_size("expert")
     n_dp = lax.axis_size("dp")
     tok_rows, model = tokens.shape
     width = model // n_dp
-    hidden = gate_weight.shape[2]
-    quarter = hidden // n_dp
     slots = min(tok_rows, 3 * tok_rows * ids.shape[1] // (2 * experts))
     gate, up, down = gate_weight[0], up_weight[0], down_weight[0]
 
@@ -112,26 +367,8 @@
     whole, grad, tab = dispatch(tokens, out_grad, table)
     x_rows, g_rows = pick_rows(whole, slots, experts, n_dp, tok_rows, width)
 
-    rows = x_rows.shape[0]
-    part = jnp.stack(
-        [
-            dot32(x_rows, gate, ((1,), (0,))).astype(BF),
-            dot32(x_rows, up, ((1,), (0,))).astype(BF),
-            dot32(g_rows, down, ((1,), (1,))).astype(BF),
-        ]
-    )
-    part = part.reshape(3, rows, n_dp, quarter).transpose(2, 1, 0, 3).reshape(n_dp * rows, 3 * quarter)
-    pre = lax.psum_scatter(part, "dp", scatter_dimension=0, tiled=True)
-    acts = activations(pre, quarter)
-    terms = lax.all_gather(acts, "dp", axis=0, tiled=False)
-    terms = terms.reshape(n_dp, rows, 3, quarter).transpose(2, 1, 0, 3).reshape(3, rows, hidden)
+    back, terms = exchange(x_rows, g_rows, gate, up, down, experts, n_dp)
     hid, gterm, uterm = terms[0], terms[1], terms[2]
-
-    out_rows = dot32(hid, down, ((1,), (0,))).astype(BF)
-    in_rows = (dot32(gterm, gate, ((1,), (1,))) + dot32(uterm, up, ((1,), (1,)))).astype(BF)
-    send = jnp.concatenate([out_rows, in_rows], axis=1).reshape(experts, n_dp * slots, 2 * width)
-    back = lax.all_to_all(send, "expert", split_axis=0, concat_axis=0, tiled=True)
-    back = back.reshape(experts * n_dp * slots, 2 * width)
 
     gate_grad = dot32(x_rows, gterm, ((0,), (0,))).astype(BF)[None]
     up_grad = dot32(x_rows, uterm, ((0,), (0,))).astype(BF)[None]

time: 521 us -> 397 us (0.76); the launches traced: 510 us -> 393 us
  waiting for transfers between devices: 317 us -> 72.5 us
  Pallas kernels: 0 us -> 222 us
  local copies, waits for them, and re-layouts: 62 us -> 9.6 us
  matrix products: 56.3 us -> 34.8 us
  other arithmetic: 22.1 us -> 8.42 us
  starting transfers between devices: 26.7 us -> 19.6 us
    pallas_call x0 -> x1, Pallas kernels: none -> 222 us  [exchange(): pl.pallas_call(functools.partial(exchange_kernel, rows // experts), out_s...]
    all_gather x1 -> x0, waiting for transfers between devices: 93 us -> none  [per_device(): terms = lax.all_gather(acts, 'dp', axis=0, tiled=False)]
    reduce_scatter x1 -> x0, waiting for transfers between devices: 87.8 us -> none  [per_device(): pre = lax.psum_scatter(part, 'dp', scatter_dimension=0, tiled=True)]
    all_to_all x1 -> x0, waiting for transfers between devices: 61.8 us -> none  [per_device(): lax.all_to_all(send, 'expert', split_axis=0, concat_axis=0, tiled=True)]
    dot_general x11 -> x5, matrix products: 45.9 us -> 24 us  [dot32(): return lax.dot_general(a, b, (dims, ((), ())), preferred_element_type=F32)]
    reshape x1 -> x0, local copies, waits for them, and re-layouts: 15.5 us -> none  [per_device(): terms.reshape(n_dp, rows, 3, quarter).transpose(2, 1, 0, 3)]
    unnamed x31 -> x10, local copies, waits for them, and re-layouts: 18.1 us -> 2.91 us
    another operation x3 -> x2, other arithmetic: 9.25 us -> 0.02 us  [the longest x1 9.23 us: per_device(): jnp.stack([dot32(x_rows, gate, ((1,), (0,))).astype(BF), dot32(x_rows, up...]
  transfers between devices with their start and end apart: 9 -> 6, of which waited for: 6 -> 3; matrix products, arithmetic and copies ran while one was open for 6% -> 5% of each run, Pallas kernels for 0% -> 0%
where the time goes in v2:
time: 397 us; the launch traced here: 393 us
  Pallas kernels  222 us (56%)
  waiting for transfers between devices  72.5 us (18%)
  matrix products  34.8 us (9%)
  starting transfers between devices  19.6 us (5%)
  between operations  14.2 us (4%)
  blocking collectives  11.9 us (3%)
  local copies, waits for them, and re-layouts  9.6 us (2%)
  other arithmetic  8.42 us (2%)
    pallas_call x1, Pallas kernels, exchange(): pl.pallas_call(functools.partial(exchange_kernel, rows // experts), out_s...  222 us
    all_gather x1, waiting for transfers between devices, dispatch(): lax.all_gather(jnp.concatenate([tok, grad, tab], axis=1), 'expert', axis=...  69.5 us
    dot_general x5, matrix products, dot32(): return lax.dot_general(a, b, (dims, ((), ())), preferred_element_type=F32)  24 us
    all_gather x1, blocking collectives, dispatch(): tab = lax.all_gather(table, 'dp', axis=0, tiled=True)  11.9 us
    all_to_all x2, starting transfers between devices, to_slices(): return lax.all_to_all(array, 'dp', split_axis=1, concat_axis=0, tiled=True)  9.64 us
  transfers between devices with their start and end apart: 6, of which 3 were waited for; matrix products, arithmetic and copies ran while one was open for 5% of the time, Pallas kernels for 0%

profile of v2, /device:TPU:34, one launch (start us, length us, event | category | flops | bytes accessed | tf_op | source)
XLA Modules:
  0.0 393.4 jit_solution(13198606570323772954)
XLA Ops:
  7.2 1.6 copy.64
  8.8 4.8 %all-to-all-start.1 = ((bf16[32,4,896]{2,0,1:T(8,128)(2,1)}), bf16[32,4,896]{2,0,1:T(8,128)(2,1)S(1)}, u32[]{:S(2)}, u32[]{:S(2)}) async-start(bf16[32,4,896]{2,0,1:T(8,128)(2,1)} %bitcast.69), calls=%async_computation.1 | async-start | bytes 458752 | tf_op jit(solution)/shard_map/all_to_all | solution.py:32
  15.3 1.6 copy.65
  17.1 1.5 all-to-all-done.1
  18.7 4.8 %all-to-all-start = ((bf16[32,4,896]{2,0,1:T(8,128)(2,1)}), bf16[32,4,896]{2,0,1:T(8,128)(2,1)S(1)}, u32[]{:S(2)}, u32[]{:S(2)}) async-start(bf16[32,4,896]{2,0,1:T(8,128)(2,1)} %bitcast.70), calls=%async_computation | async-start | bytes 458752 | tf_op jit(solution)/shard_map/all_to_all | solution.py:32
  23.6 11.9 %all_gather.9 = bf16[128,128]{1,0:T(8,128)(2,1)S(1)} all-gather(bf16[32,128]{1,0:T(8,128)(2,1)S(1)} %pad_maximum_fusion.1), channel_id=1, replica_groups=mesh['dp'=4,'expert'=32] {'dp'}, dimensions={0}, use_global_device_ids=true | all-gather | bytes 40960 | tf_op jit(solution)/shard_map/all_gather | solution.py:39
  35.5 0.8 pad_maximum_fusion
  37.2 1.2 bitcast_select_fusion
  38.4 69.5 %all-gather.3.cloned.1.call-done = bf16[4096,1920]{1,0:T(8,128)(2,1)} async-done(((bf16[128,1920]{1,0:T(8,128)(2,1)}), bf16[4096,1920]{1,0:T(8,128)(2,1)}) %all-gather.3.cloned.1.call-update) | async-done | bytes 15728656 | tf_op jit(solution)/shard_map/all_gather | solution.py:40
  108.0 2.0 fusion.19
  109.9 6.5 %fusion = f32[32,48,1792]{2,1,0:T(8,128)S(1)} fusion(bf16[32,128,1920]{2,1,0:T(8,128)(2,1)} %bitcast.72, f32[32,128]{1,0:T(8,128)S(1)} %get-tuple-element.17, f32[48]{0:T(128)S(1)} %fusion.40, pred[48,128]{1,0:T(8,128)(4,1)S(1)} %broadcast_compare_fusion), kind=kOutput, calls=%fused_computation | convolution fusion | flops 705036288 | bytes 25712832 | tf_op jit(solution)/shard_map/dot_general | solution.py:57
  116.9 1.8 slice.102
  118.7 1.9 fusion.2
  120.6 222.3 %shard_map.118 = (bf16[1536,1792]{1,0:T(8,128)(2,1)}, bf16[3,1536,1024]{2,1,0:T(8,128)(2,1)}) custom-call(bf16[1536,896]{1,0:T(8,128)(2,1)} %bitcast.73, bf16[1536,896]{1,0:T(8,128)(2,1)} %bitcast.76, bf16[896,1024]{1,0:T(8,128)(2,1)} %bitcast.78, bf16[896,1024]{1,0:T(8,128)(2,1)} %bitcast.79, bf16[1024,896]{1,0:T(8,128)(2,1)} %bitcast.80), custom_call_target="tpu_custom_call" | custom-call | tf_op jit(solution)/shard_map/pallas_call | solution.py:331
  342.9 7.6 %convert_bitcast_fusion = bf16[1,1024,896]{2,1,0:T(8,128)(2,1)} fusion(bf16[1536,896]{1,0:T(8,128)(2,1)} %bitcast.77, bf16[3,1536,1024]{2,1,0:T(8,128)(2,1)} %get-tuple-element.9), kind=kOutput, calls=%fused_computation.24 | convolution fusion | flops 2819489792 | bytes 7733248 | tf_op jit(solution)/shard_map/dot_general | solution.py:16
  350.5 6.3 %convert_bitcast_fusion.1 = bf16[1,896,1024]{2,1,0:T(8,128)(2,1)} fusion(bf16[1536,896]{1,0:T(8,128)(2,1)S(1)} %bitcast.74, bf16[3,1536,1024]{2,1,0:T(8,128)(2,1)} %get-tuple-element.9), kind=kOutput, calls=%fused_computation.25 | convolution fusion | flops 2819489792 | bytes 7733248 | tf_op jit(solution)/shard_map/dot_general | solution.py:16
  356.8 0.9 fusion.14
  358.7 3.1 fusion.29
  361.8 5.1 %all-to-all-start.3 = ((bf16[4,32,896]{2,1,0:T(8,128)(2,1)}), bf16[4,32,896]{2,1,0:T(8,128)(2,1)S(1)}, u32[]{:S(2)}, u32[]{:S(2)}) async-start(bf16[4,32,896]{2,1,0:T(8,128)(2,1)} %bitcast.15), calls=%async_computation.3 | async-start | bytes 458752 | tf_op jit(solution)/shard_map/all_to_all | solution.py:86
  367.0 4.2 %fusion.26 = bf16[128,896]{1,0:T(8,128)(2,1)} fusion(f32[128,1536]{0,1:T(8,128)} %bitcast_select_fusion, bf16[1536,1792]{1,0:T(8,128)(2,1)} %get-tuple-element.8), kind=kOutput, calls=%fused_computation.27 | convolution fusion | flops 2114043904 | bytes 3768320 | tf_op jit(solution)/shard_map/dot_general | solution.py:79
  371.2 1.4 all-to-all-done.3
  372.6 4.8 %all-to-all-start.2 = ((bf16[4,32,896]{2,1,0:T(8,128)(2,1)}), bf16[4,32,896]{2,1,0:T(8,128)(2,1)S(1)}, u32[]{:S(2)}, u32[]{:S(2)}) async-start(bf16[4,32,896]{2,1,0:T(8,128)(2,1)} %bitcast.13), calls=%async_computation.2 | async-start | bytes 458752 | tf_op jit(solution)/shard_map/all_to_all | solution.py:85
  377.4 6.2 %convert_bitcast_fusion.2 = bf16[1,896,1024]{2,1,0:T(8,128)(2,1)} fusion(bf16[1536,896]{1,0:T(8,128)(2,1)S(1)} %bitcast.75, bf16[3,1536,1024]{2,1,0:T(8,128)(2,1)} %get-tuple-element.9), kind=kOutput, calls=%fused_computation.26 | convolution fusion | flops 2819489792 | bytes 7733248 | tf_op jit(solution)/shard_map/dot_general | solution.py:16
  383.6 0.9 select_reduce_fusion.2
  (42 shorter events, 6.3 us)
Async XLA Ops:
  8.8 9.9 %all-to-all-start.1 = ((bf16[32,4,896]{2,0,1:T(8,128)(2,1)}), bf16[32,4,896]{2,0,1:T(8,128)(2,1)S(1)}, u32[]{:S(2)}, u32[]{:S(2)}) async-start(bf16[32,4,896]{2,0,1:T(8,128)(2,1)} %bitcast.69), calls=%async_computation.1 | async-start | bytes 458752 | tf_op jit(solution)/shard_map/all_to_all | solution.py:32
  18.7 16.8 %all-to-all-start = ((bf16[32,4,896]{2,0,1:T(8,128)(2,1)}), bf16[32,4,896]{2,0,1:T(8,128)(2,1)S(1)}, u32[]{:S(2)}, u32[]{:S(2)}) async-start(bf16[32,4,896]{2,0,1:T(8,128)(2,1)} %bitcast.70), calls=%async_computation | async-start | bytes 458752 | tf_op jit(solution)/shard_map/all_to_all | solution.py:32
  23.5 84.5 %all-gather.3.cloned.1.call-start = ((), (), s32[]{:S(2)}) async-start(), calls=%async_computation.5 | async-start | bytes 16220160 | tf_op jit(solution)/shard_map/all_gather | solution.py:40
  36.4 347.2 %reduce-scatter.4.cloned.1.call-start = ((), (), s32[]{:S(2)}) async-start(), calls=%async_computation.6 | async-start | bytes 81920 | tf_op jit(solution)/shard_map/reduce_scatter | solution.py:87
  342.9 7.6 %copy-start = (bf16[32,48,896]{2,1,0:T(8,128)(2,1)S(1)}, bf16[32,48,896]{2,1,0:T(8,128)(2,1)}, u32[]{:S(2)}) copy-start(bf16[32,48,896]{2,1,0:T(8,128)(2,1)} %slice.102) | copy-start | bytes 8257540
  342.9 13.9 %slice-start = ((s8[5505024]{0:T(1024)(128)(4,1)}), s8[4194304]{0:T(1024)(128)(4,1)S(1)}, s32[]{:S(2)}) async-start(s8[5505024]{0:T(1024)(128)(4,1)} %bitcast.91), calls=%async_computation.7 | async-start | bytes 8388608
  350.5 6.3 %slice-start.1 = ((s8[5505024]{0:T(1024)(128)(4,1)}), s8[1310720]{0:T(1024)(128)(4,1)S(1)}, s32[]{:S(2)}) async-start(s8[5505024]{0:T(1024)(128)(4,1)} %bitcast.91), calls=%async_computation.8 | async-start | bytes 2621440
  361.8 10.8 %all-to-all-start.3 = ((bf16[4,32,896]{2,1,0:T(8,128)(2,1)}), bf16[4,32,896]{2,1,0:T(8,128)(2,1)S(1)}, u32[]{:S(2)}, u32[]{:S(2)}) async-start(bf16[4,32,896]{2,1,0:T(8,128)(2,1)} %bitcast.15), calls=%async_computation.3 | async-start | bytes 458752 | tf_op jit(solution)/shard_map/all_to_all | solution.py:86
  372.6 13.3 %all-to-all-start.2 = ((bf16[4,32,896]{2,1,0:T(8,128)(2,1)}), bf16[4,32,896]{2,1,0:T(8,128)(2,1)S(1)}, u32[]{:S(2)}, u32[]{:S(2)}) async-start(bf16[4,32,896]{2,1,0:T(8,128)(2,1)} %bitcast.13), calls=%async_computation.2 | async-start | bytes 458752 | tf_op jit(solution)/shard_map/all_to_all | solution.py:85
Sparse Core Ops, SparseCore 0:
  36.5 71.4 all-gather.2
  358.9 20.7 reduce-scatter.3

commit v3 on v2

v3 whole, which is shorter than its diff:
```python
import functools

import jax
import jax.numpy as jnp
from jax import lax
from jax.experimental import pallas as pl
from jax.experimental.pallas import tpu as pltpu
from jax.sharding import PartitionSpec as P

BF = jnp.bfloat16
F32 = jnp.float32
LANES = 128


def dot32(a, b, dims):
    return lax.dot_general(a, b, (dims, ((), ())), preferred_element_type=F32)


def route_table(ids, weights, experts):
    onehot = (ids[:, :, None] == jnp.arange(experts, dtype=jnp.int32)).astype(jnp.int32)
    chosen = jnp.sum(onehot, axis=1)
    place = jnp.cumsum(chosen, axis=0) * chosen
    dense = jnp.sum(onehot.astype(F32) * weights[:, :, None], axis=1)
    high = lax.reduce_precision(dense, 8, 7)
    middle = lax.reduce_precision(dense - high, 8, 7)
    low = dense - high - middle
    return jnp.concatenate([place.astype(F32), high, middle, low], axis=1).astype(BF)


def combine(back, ids, grad, tab, slots, experts, n_dp, tok_rows, width):
    tab = tab.astype(F32)
    toks = n_dp * tok_rows
    place = tab[:, :experts]
    weight = tab[:, experts : 2 * experts] + tab[:, 2 * experts : 3 * experts] + tab[:, 3 * experts : 4 * experts]
    row = jnp.arange(n_dp * slots, dtype=jnp.int32)
    tok = jnp.arange(toks, dtype=jnp.int32)
    same = (row[None, :] // slots) == (tok[:, None] // tok_rows)
    hit = same[:, None, :] & (place[:, :, None] == (row % slots + 1).astype(F32))
    flat = hit.reshape(toks, -1)
    scaled = jnp.where(hit, weight[:, :, None], 0.0).reshape(toks, -1)
    out_rows = back[:, :width]
    in_rows = back[:, width:]
    mixed = lax.dot_general(
        scaled, out_rows.astype(F32), (((1,), (0,)), ((), ())), precision=lax.Precision.HIGHEST
    )
    tgrad = dot32(flat.astype(BF), in_rows, ((1,), (0,)))
    dots = dot32(grad, out_rows, ((1,), (1,)))
    route = jnp.sum(jnp.where(hit, dots.reshape(hit.shape), 0.0), axis=2)
    both = jnp.concatenate([mixed, tgrad], axis=1).astype(BF).reshape(n_dp, tok_rows, 2 * width)
    both = lax.all_to_all(both, "dp", 0, 0, tiled=True)
    route = jnp.sum(lax.all_to_all(route.reshape(n_dp, tok_rows, experts), "dp", 0, 0, tiled=True), axis=0)
    both = both.transpose(1, 0, 2)
    mixed = both[:, :, :width].reshape(tok_rows, n_dp * width)
    tgrad = both[:, :, width:].reshape(tok_rows, n_dp * width)
    onehot = ids[:, :, None] == jnp.arange(experts, dtype=jnp.int32)
    route = jnp.sum(jnp.where(onehot, route[:, None, :], 0.0), axis=2)
    return mixed, tgrad, route


CHUNKS = 4
SIDE = 4
ORDER = (0, 1, 3, 2)
MESH = pl.DeviceIdType.MESH


def exchange_kernel(
    slots, tok_ref, grad_ref, tab_ref, gate_ref, up_ref, down_ref,
    back_ref, whole_ref, gate_out, up_out, down_out,
    blk, x_s, xt_s, g_s, hid_t, part, own, in_half, in_full, terms, rows_out, stage_a, stage_b,
    ring_send, ring_recv, ret_send, ret_recv, a2a_send, a2a_recv, ag_send, ag_recv,
    pair_send, pair_recv, local_sem, stage_sem,
):
    n_dp = lax.axis_size("dp")
    experts = lax.axis_size("expert")
    d = lax.axis_index("dp")
    e = lax.axis_index("expert")
    y = e // (2 * SIDE)
    z = (e // 2) % SIDE
    c = e % 2
    tok_rows = tok_ref.shape[0]
    toks = n_dp * tok_rows
    slots_dp = n_dp * slots
    group = experts // CHUNKS
    chunk = group * slots_dp
    half = chunk // 2
    quarter = own.shape[3]
    width = gate_ref.shape[0]
    to = ((d + n_dp - 1) % n_dp, (d + 1) % n_dp)

    barrier = pltpu.get_barrier_semaphore()
    for m in range(1, n_dp):
        pl.semaphore_signal(barrier, inc=1, device_id={"dp": (d + m) % n_dp}, device_id_type=MESH)

    def greet(step, carry):
        pl.semaphore_signal(
            barrier, inc=1, device_id={"expert": (e + step) % experts}, device_id_type=MESH
        )
        return carry

    lax.fori_loop(1, experts, greet, 0)
    pl.semaphore_wait(barrier, experts + n_dp - 2)

    sends = []

    def launch(item):
        item.start()
        sends.append(item)

    def spot(da, db, s):
        return db * group + s * SIDE + da

    def block(p, h=None):
        if h is None:
            return whole_ref.at[pl.ds(pl.multiple_of(p * toks, toks), toks), :]
        rows = toks // 2
        return whole_ref.at[pl.ds(pl.multiple_of(p * toks + h * rows, rows), rows), :]

    def to_slice(m, number):
        q = (d + m) % n_dp
        rows = pl.ds(pl.multiple_of((c * SIDE) * toks + d * tok_rows, tok_rows), tok_rows)
        cols = pl.ds(pl.multiple_of(q * width, LANES), width)
        source = (tok_ref.at[:, cols], grad_ref.at[:, cols], tab_ref)[number]
        target = whole_ref.at[rows, pl.ds(number * width, LANES if number == 2 else width)]
        if m == 0:
            return pltpu.make_async_copy(source, target, local_sem.at[number])
        return pltpu.make_async_remote_copy(
            src_ref=source, dst_ref=target, send_sem=a2a_send.at[m - 1, number],
            recv_sem=a2a_recv.at[m - 1, number], device_id={"dp": q}, device_id_type=MESH,
        )

    def from_slice(m, number):
        rows = pl.ds(pl.multiple_of((c * SIDE) * toks + ((d + n_dp - m) % n_dp) * tok_rows, tok_rows), tok_rows)
        ref = whole_ref.at[rows, pl.ds(number * width, LANES if number == 2 else width)]
        return pltpu.make_async_remote_copy(
            src_ref=ref, dst_ref=ref, send_sem=a2a_send.at[m - 1, number],
            recv_sem=a2a_recv.at[m - 1, number], device_id={"dp": (d + m) % n_dp}, device_id_type=MESH,
        )

    def ag_copy_to(axis, way, da, db, h):
        step = SIDE - 1 if way == 0 else 1
        seen = 1 if way == 0 else SIDE - 1
        da2 = (da + seen) % SIDE if axis == 0 else da
        db2 = (db + seen) % SIDE if axis == 1 else db
        along_y = 1 - c if axis == 0 else c
        y2 = (y + step * along_y) % SIDE
        z2 = (z + step * (1 - along_y)) % SIDE
        p2 = spot(da2, db2, c)
        return pltpu.make_async_remote_copy(
            src_ref=block(spot(da, db, c), h),
            dst_ref=block(p2, h),
            send_sem=ag_send.at[da * SIDE + db, axis * 2 + way, h],
            recv_sem=ag_recv.at[da2 * SIDE + db2, h],
            device_id={"expert": (y2 * SIDE + z2) * 2 + c},
            device_id_type=MESH,
        )

    def ag_wait(da, db, h):
        ref = block(spot(da, db, c), h)
        pltpu.make_async_remote_copy(
            src_ref=ref, dst_ref=ref, send_sem=ag_send.at[0, 0, 0], recv_sem=ag_recv.at[da * SIDE + db, h],
            device_id={"expert": (e + 1) % experts}, device_id_type=MESH,
        ).wait_recv()

    def pair_copy(da, db, s):
        ref = block(spot(da, db, s))
        return pltpu.make_async_remote_copy(
            src_ref=ref, dst_ref=ref, send_sem=pair_send.at[da * SIDE + db], recv_sem=pair_recv.at[da * SIDE + db],
            device_id={"expert": e + 1 - 2 * c}, device_id_type=MESH,
        )

    def spread(axis, da, db):
        for way, h in ((0, 0), (1, 1), (0, 1), (1, 0)):
            launch(ag_copy_to(axis, way, da, db, h))

    def slices():
        for m in range(n_dp):
            for number in range(3):
                to_slice(m, number).start()
        for number in range(3):
            to_slice(0, number).wait()
            for m in range(1, n_dp):
                from_slice(m, number).wait_recv()

    def first_phase():
        spread(0, 0, 0)
        launch(pair_copy(0, 0, c))
        ag_wait(1, 0, 0)
        launch(ag_copy_to(0, 0, 1, 0, 0))
        ag_wait(3, 0, 1)
        launch(ag_copy_to(0, 1, 3, 0, 1))
        spread(1, 0, 0)
        for da in (1, 3):
            ag_wait(da, 0, 1 if da == 1 else 0)
            launch(pair_copy(da, 0, c))
            spread(1, da, 0)
        ag_wait(2, 0, 0)
        ag_wait(2, 0, 1)
        launch(pair_copy(2, 0, c))
        spread(1, 2, 0)

    def second_phase(da):
        ag_wait(da, 1, 0)
        launch(ag_copy_to(1, 0, da, 1, 0))
        ag_wait(da, 3, 1)
        launch(ag_copy_to(1, 1, da, 3, 1))
        ag_wait(da, 1, 1)
        launch(pair_copy(da, 1, c))
        ag_wait(da, 3, 0)
        launch(pair_copy(da, 3, c))

    def third_phase(da):
        ag_wait(da, 2, 0)
        ag_wait(da, 2, 1)
        launch(pair_copy(da, 2, c))

    def take_chunk(k):
        db = ORDER[k]
        for da in range(SIDE):
            pair_copy(da, db, 1 - c).wait_recv()
        load = pltpu.make_async_copy(
            whole_ref.at[pl.ds(db * group * toks, group * toks), :], blk, local_sem.at[3]
        )
        load.start()
        load.wait()
        pair_rows = 2 * slots_dp
        pair_toks = 2 * toks

        def one(i, carry):
            span = pl.ds(pl.multiple_of(i * pair_toks, pair_toks), pair_toks)
            line = lax.broadcasted_iota(jnp.int32, (16, LANES), 0)
            lane = lax.broadcasted_iota(jnp.int32, (16, LANES), 1)
            want = jnp.where((lane == line * experts + e) & (line < 4), 1.0, 0.0).astype(BF)
            found = dot32(want, blk[span, 2 * width :], ((1,), (1,)))
            place = found[0:1, :]
            scale = found[1:2, :] + found[2:3, :] + found[3:4, :]
            token = lax.broadcasted_iota(jnp.int32, (1, pair_toks), 1)
            base = (lax.shift_right_logical(token, tok_rows.bit_length() - 1) * slots).astype(F32)
            goal = jnp.where(place > 0.0, base + place - 1.0, -1.0)
            row = lax.broadcasted_iota(jnp.int32, (pair_rows, pair_toks), 0).astype(F32)
            hit = row == goal
            picked = jnp.dot(
                jnp.where(hit, 1.0, 0.0).astype(BF), blk[span, : 2 * width], preferred_element_type=F32
            )
            scales = jnp.sum(jnp.where(hit, scale, 0.0), axis=1, keepdims=True)
            x_s[pl.ds(pl.multiple_of(i * pair_rows, pair_rows), pair_rows), :] = picked[:, :width].astype(BF)
            g_s[pl.ds(pl.multiple_of(k * chunk + i * pair_rows, pair_rows), pair_rows), :] = (
                picked[:, width:] * scales
            ).astype(BF)
            return carry

        lax.fori_loop(0, group // 2, one, 0)

    def rows_of(k, part_half=None):
        if part_half is None:
            return pl.ds(k * chunk, chunk)
        return pl.ds(k * chunk + part_half * half, half)

    def cols_of(q):
        return pl.ds(pl.multiple_of(q * quarter, quarter), quarter)

    def copy(k, way, number, source, target):
        return pltpu.make_async_remote_copy(
            src_ref=source,
            dst_ref=target,
            send_sem=ring_send.at[k, way, number],
            recv_sem=ring_recv.at[k, way, number],
            device_id={"dp": to[way]},
            device_id_type=MESH,
        )

    def toward(k, way):
        return part.at[k, 2 if way == 0 else 0]

    def halves(ref, h):
        return ref.at[:, pl.ds(h * half, half), :]

    def rs_copy(k, way, number):
        if number == 0:
            return copy(k, way, 0, halves(part.at[k, 1], way), in_half.at[k, way])
        h = way if number == 2 else 1 - way
        return copy(k, way, number, halves(toward(k, way), h), halves(in_full.at[k, way], h))

    def ag_copy(k, way, number):
        if number == 5:
            q = (d + 1) % n_dp if way == 0 else (d + n_dp - 1) % n_dp
            h = way
        else:
            q = d
            h = way if number == 3 else 1 - way
        ref = terms.at[:, rows_of(k, h), cols_of(q)]
        return copy(k, way, number, ref, ref)

    def ag_arrival(k, way, number):
        src = (d + 1) % n_dp if way == 0 else (d + n_dp - 1) % n_dp
        q = (d + 2) % n_dp if number == 5 else src
        h = way if number in (3, 5) else 1 - way
        ref = terms.at[:, rows_of(k, h), cols_of(q)]
        return copy(k, way, number, ref, ref)

    def partial(k, q, i):
        if i == 0:
            return jnp.dot(x_s[...], gate_ref[:, cols_of(q)], preferred_element_type=F32)
        if i == 1:
            return jnp.dot(x_s[...], up_ref[:, cols_of(q)], preferred_element_type=F32)
        return dot32(g_s[rows_of(k), :], down_ref[cols_of(q), :], ((1,), (1,)))

    def stage0(k):
        def one(step, carry):
            m = (step + 1) % (n_dp - 1)
            q = (d + m + 1) % n_dp
            for i in range(3):
                part[k, m, i] = partial(k, q, i).astype(BF)
            return carry

        lax.fori_loop(0, n_dp - 1, one, 0)
        for way in range(2):
            rs_copy(k, way, 0).start()
        for way in range(2):
            rs_copy(k, way, 1).start()
        for i in range(3):
            own[k, i] = partial(k, d, i)
        xt_s[:, rows_of(k)] = x_s[...].T

    def stage1(k):
        for way in range(2):
            rs_copy(k, way, 0).wait_recv()
            m = 2 if way == 0 else 0
            for i in range(3):
                span = pl.ds(way * half, half)
                total = part[k, m, i, span, :].astype(F32) + in_half[k, way, i].astype(F32)
                part[k, m, i, span, :] = total.astype(BF)
            rs_copy(k, way, 2).start()

    def stage2(k):
        for number in (1, 2):
            for way in range(2):
                rs_copy(k, way, number).wait_recv()

        def total(i, span):
            return own[k, i, span, :] + in_full[k, 0, i, span, :].astype(F32) + in_full[k, 1, i, span, :].astype(F32)

        step_rows = half // 2

        def act(step, carry):
            span = pl.ds(pl.multiple_of(step * step_rows, step_rows), step_rows)
            gate = total(0, span)
            up = total(1, span)
            hgrad = total(2, span)
            sig = jax.nn.sigmoid(gate)
            val = gate * sig
            slope = sig * (1.0 + gate * (1.0 - sig))
            target = pl.ds(pl.multiple_of(k * chunk + step * step_rows, step_rows), step_rows)
            terms[0, target, cols_of(d)] = (val * up).astype(BF)
            terms[1, target, cols_of(d)] = (hgrad * up * slope).astype(BF)
            terms[2, target, cols_of(d)] = (hgrad * val).astype(BF)
            return carry

        lax.fori_loop(0, chunk // step_rows, act, 0)
        for number in (3, 4):
            for way in range(2):
                ag_copy(k, way, number).start()

    def stage3(k):
        for way in range(2):
            ag_arrival(k, way, 3).wait_recv()
            ag_copy(k, way, 5).start()

    def home(p):
        return pl.ds(pl.multiple_of(p * slots_dp, slots_dp), slots_dp)

    def back_copy(k, i):
        db = ORDER[k]
        s = i // SIDE
        da = i % SIDE
        y2 = (y + da * (1 - s) + db * s) % SIDE
        z2 = (z + db * (1 - s) + da * s) % SIDE
        j = (y2 * SIDE + z2) * 2 + s
        return pltpu.make_async_remote_copy(
            src_ref=rows_out.at[home(k * group + i), :],
            dst_ref=back_ref.at[home(e), :],
            send_sem=ret_send.at[k * group + i],
            recv_sem=ret_recv.at[e],
            device_id={"expert": j},
            device_id_type=MESH,
        )

    def self_copy():
        return pltpu.make_async_copy(
            rows_out.at[home(c * SIDE), :], back_ref.at[home(e), :], local_sem.at[4]
        )

    def each_back(k, act):
        def one(step, carry):
            act(back_copy(k, (c * SIDE + step) % group))
            return carry

        lax.fori_loop(1 if k == 0 else 0, group, one, 0)

    def stage4(k):
        for way in range(2):
            ag_arrival(k, way, 4).wait_recv()
        for way in range(2):
            ag_arrival(k, way, 5).wait_recv()

        def one(h, carry):
            span = pl.ds(pl.multiple_of(k * chunk + h * half, half), half)
            rows_out[span, :width] = jnp.dot(
                terms[0, span, :], down_ref[...], preferred_element_type=F32
            ).astype(BF)
            rows_out[span, width:] = (
                dot32(terms[1, span, :], gate_ref[...], ((1,), (1,)))
                + dot32(terms[2, span, :], up_ref[...], ((1,), (1,)))
            ).astype(BF)
            return carry

        lax.fori_loop(0, 2, one, 0)
        if k == 0:
            self_copy().start()
        each_back(k, lambda item: item.start())
        hid_t[:, rows_of(k)] = terms[0, rows_of(k), :].T

    def weight_grads():
        span = stage_a.shape[2]
        tall = stage_b.shape[1]

        def out_copy(kind, i, slot):
            if kind == 2:
                target = down_out.at[pl.ds(pl.multiple_of(i * tall, tall), tall), :]
                return pltpu.make_async_copy(stage_b.at[slot], target, stage_sem.at[kind, slot])
            target = (gate_out, up_out)[kind].at[:, pl.ds(pl.multiple_of(i * span, span), span)]
            return pltpu.make_async_copy(stage_a.at[slot], target, stage_sem.at[kind, slot])

        for kind in range(3):
            count = gate_ref.shape[1] // (tall if kind == 2 else span)

            def one(i, carry, kind=kind):
                slot = i % 2

                @pl.when(i >= 2)
                def _():
                    out_copy(kind, i - 2, slot).wait()

                if kind == 2:
                    left = hid_t[pl.ds(pl.multiple_of(i * tall, tall), tall), :]
                    stage_b[slot] = jnp.dot(left, g_s[...], preferred_element_type=F32).astype(BF)
                else:
                    right = terms[1 + kind, :, pl.ds(pl.multiple_of(i * span, span), span)]
                    stage_a[slot] = jnp.dot(xt_s[...], right, preferred_element_type=F32).astype(BF)
                out_copy(kind, i, slot).start()
                return carry

            lax.fori_loop(0, count, one, 0)
            out_copy(kind, count - 2, count % 2).wait()
            out_copy(kind, count - 1, (count - 1) % 2).wait()

    slices()
    first_phase()
    for t in range(CHUNKS + 4):
        if 0 <= t - 1 < CHUNKS:
            stage1(t - 1)
        if t == 1:
            second_phase(3)
            second_phase(2)
        if 0 <= t - 2 < CHUNKS:
            stage2(t - 2)
        if 0 <= t - 3 < CHUNKS:
            stage3(t - 3)
        if t == 2:
            for da in (0, 1, 3, 2):
                third_phase(da)
        if t < CHUNKS:
            take_chunk(t)
            stage0(t)
        if t == 0:
            second_phase(0)
            second_phase(1)
        if 0 <= t - 4 < CHUNKS:
            stage4(t - 4)
    weight_grads()

    for m in range(1, n_dp):
        for number in range(3):
            to_slice(m, number).wait_send()
    for item in sends:
        item.wait_send()
    for k in range(CHUNKS):
        for way in range(2):
            for number in range(3):
                rs_copy(k, way, number).wait_send()
                ag_copy(k, way, number + 3).wait_send()
        each_back(k, lambda item: item.wait_send())
    self_copy().wait()

    def arrived(step, carry):
        s = (e + step) % experts
        ref = back_ref.at[home(s), :]
        pltpu.make_async_remote_copy(
            src_ref=ref, dst_ref=ref, send_sem=ret_send.at[s], recv_sem=ret_recv.at[s],
            device_id={"expert": s}, device_id_type=MESH,
        ).wait_recv()
        return carry

    lax.fori_loop(1, experts, arrived, 0)


def exchange(tokens, out_grad, table, gate, up, down, slots, experts, n_dp):
    width, hidden = gate.shape
    toks = n_dp * tokens.shape[0]
    rows = experts * n_dp * slots
    quarter = hidden // n_dp
    chunk = rows // CHUNKS
    group = experts // CHUNKS
    dma = pltpu.SemaphoreType.DMA
    anywhere = pl.BlockSpec(memory_space=pl.ANY)
    return pl.pallas_call(
        functools.partial(exchange_kernel, slots),
        out_shape=(
            jax.ShapeDtypeStruct((rows, 2 * width), BF),
            jax.ShapeDtypeStruct((experts * toks, 2 * width + LANES), BF),
            jax.ShapeDtypeStruct((width, hidden), BF),
            jax.ShapeDtypeStruct((width, hidden), BF),
            jax.ShapeDtypeStruct((hidden, width), BF),
        ),
        in_specs=[pl.BlockSpec(memory_space=pltpu.VMEM)] * 6,
        out_specs=(anywhere,) * 5,
        scratch_shapes=[
            pltpu.VMEM((group * toks, 2 * width + LANES), BF),
            pltpu.VMEM((chunk, width), BF),
            pltpu.VMEM((width, rows), BF),
            pltpu.VMEM((rows, width), BF),
            pltpu.VMEM((hidden, rows), BF),
            pltpu.VMEM((CHUNKS, n_dp - 1, 3, chunk, quarter), BF),
            pltpu.VMEM((CHUNKS, 3, chunk, quarter), F32),
            pltpu.VMEM((CHUNKS, 2, 3, chunk // 2, quarter), BF),
            pltpu.VMEM((CHUNKS, 2, 3, chunk, quarter), BF),
            pltpu.VMEM((3, rows, hidden), BF),
            pltpu.VMEM((rows, 2 * width), BF),
            pltpu.VMEM((2, width, quarter), BF),
            pltpu.VMEM((2, quarter, width), BF),
            dma((CHUNKS, 2, 6)),
            dma((CHUNKS, 2, 6)),
            dma((experts,)),
            dma((experts,)),
            dma((n_dp - 1, 3)),
            dma((n_dp - 1, 3)),
            dma((SIDE * SIDE, 4, 2)),
            dma((SIDE * SIDE, 2)),
            dma((SIDE * SIDE,)),
            dma((SIDE * SIDE,)),
            dma((5,)),
            dma((3, 2)),
        ],
        compiler_params=pltpu.CompilerParams(
            collective_id=0, has_side_effects=True, vmem_limit_bytes=63 * 1024 * 1024
        ),
    )(tokens, out_grad, table, gate, up, down)


def per_device(tokens, ids, weights, out_grad, gate_weight, up_weight, down_weight):
    experts = lax.axis_size("expert")
    n_dp = lax.axis_size("dp")
    tok_rows, model = tokens.shape
    width = model // n_dp
    slots = min(tok_rows, 3 * tok_rows * ids.shape[1] // (2 * experts))
    gate, up, down = gate_weight[0], up_weight[0], down_weight[0]

    table = route_table(ids, weights, experts)
    back, whole, gate_grad, up_grad, down_grad = exchange(
        tokens, out_grad, table, gate, up, down, slots, experts, n_dp
    )
    mine = (lax.axis_index("expert") % 2) * SIDE * n_dp * tok_rows
    block = lax.dynamic_slice_in_dim(whole, mine, n_dp * tok_rows, 0)
    grad, tab = block[:, width : 2 * width], block[:, 2 * width :]
    mixed, tgrad, route = combine(back, ids, grad, tab, slots, experts, n_dp, tok_rows, width)
    return (mixed, tgrad, route, gate_grad[None], up_grad[None], down_grad[None])


def solution(mesh):
    rows = P(("dp", "expert"), None)
    weights = (P("expert", "dp", None), P("expert", "dp", None), P("expert", None, "dp"))
    return jax.shard_map(
        per_device,
        mesh=mesh,
        in_specs=(rows, rows, rows, rows) + weights,
        out_specs=(rows, rows, rows) + weights,
        check_vma=False,
    )
```

time: 397 us -> 297 us (0.75)
  waiting for transfers between devices: 72.5 us -> 4.05 us
  matrix products: 34.8 us -> 8.48 us
  Pallas kernels: 222 us -> 248 us
  between operations: 14.2 us -> 0.83 us
  blocking collectives: 11.9 us -> 0 us
  starting transfers between devices: 19.6 us -> 8.91 us
  local copies, waits for them, and re-layouts: 9.6 us -> 17 us
  other arithmetic: 8.42 us -> 4.12 us
    all_gather x1 -> x0, waiting for transfers between devices: 69.5 us -> none  [dispatch(): lax.all_gather(jnp.concatenate([tok, grad, tab], axis=1), 'expert', axis=...]
    pallas_call x1, Pallas kernels: 222 us -> 248 us  [exchange(): pl.pallas_call(functools.partial(exchange_kernel, slots), out_shape=(jax....]
    dot_general x5 -> x2, matrix products: 24 us -> 5.25 us  [dot32(): return lax.dot_general(a, b, (dims, ((), ())), preferred_element_type=F32)]
    all_gather x1 -> x0, blocking collectives: 11.9 us -> none  [dispatch(): tab = lax.all_gather(table, 'dp', axis=0, tiled=True)]
    all_to_all x4 -> x2, starting transfers between devices: 19.6 us -> 8.91 us  [the longest x1 4.8 us: combine(): both = lax.all_to_all(both, 'dp', 0, 0, tiled=True)]
    dot_general x1 -> x0, matrix products: 6.54 us -> none  [pick_rows(): lax.dot_general(hit.astype(BF), whole[:, :, :2 * width], (((2,), (1,)), (...]
    unnamed x10 -> x18, local copies, waits for them, and re-layouts: 2.91 us -> 7.76 us
  transfers between devices with their start and end apart: 6 -> 2, of which waited for: 3 -> 1; matrix products, arithmetic and copies ran while one was open for 5% -> 5% of each run, Pallas kernels for 0% -> 0%
where the time goes in v3:
time: 297 us; the launch traced here: 291 us
  Pallas kernels  248 us (84%)
  local copies, waits for them, and re-layouts  17 us (6%)
  starting transfers between devices  8.91 us (3%)
  matrix products  8.48 us (3%)
  other arithmetic  4.12 us (1%)
  waiting for transfers between devices  4.05 us (1%)
    pallas_call x1, Pallas kernels, exchange(): pl.pallas_call(functools.partial(exchange_kernel, slots), out_shape=(jax....  248 us
    unnamed x18, local copies, waits for them, and re-layouts  7.76 us
  transfers between devices with their start and end apart: 2, of which 1 were waited for; matrix products, arithmetic and copies ran while one was open for 5% of the time, Pallas kernels for 0%

profile of v3, /device:TPU:34, one launch (start us, length us, event | category | flops | bytes accessed | tf_op | source)
XLA Modules:
  0.0 291.3 jit_solution(8122608336349781157)
XLA Ops:
  0.7 0.8 copy.43
  1.6 0.8 copy.44
  2.6 0.7 pad_maximum_fusion.1.tab_ref
  3.3 248.0 %shard_map.118 = (bf16[1536,1792]{1,0:T(8,128)(2,1)}, bf16[4096,1920]{1,0:T(8,128)(2,1)}, bf16[896,1024]{1,0:T(8,128)(2,1)}, bf16[896,1024]{1,0:T(8,128)(2,1)}, bf16[1024,896]{1,0:T(8,128)(2,1)}) custom-call(bf16[32,3584]{1,0:T(8,128)(2,1)} %tok_ref.1, bf16[32,3584]{1,0:T(8,128)(2,1)} %grad_ref.1, bf16[32,128]{1,0:T(8,128)(2,1)} %pad_maximum_fusion.1.tab_ref, ...), custom_call_target="tpu_custom_call" | custom-call | tf_op jit(solution)/shard_map/pallas_call | solution.py:515
  251.2 0.8 dynamic-slice_convert_fusion
  252.2 2.8 fusion.5
  255.5 0.7 reshape.158
  256.2 4.1 %all-to-all-start.1 = ((f32[4,1,1024]{2,1,0:T(1,128)}), f32[4,1,1024]{2,1,0:T(1,128)S(1)}, u32[]{:S(2)}, u32[]{:S(2)}) async-start(f32[4,1,1024]{2,1,0:T(1,128)} %reshape.158), calls=%async_computation.1 | async-start | bytes 32768 | tf_op jit(solution)/shard_map/all_to_all | solution.py:51
  261.0 1.8 eq.81
  262.9 1.2 and.65
  264.8 2.7 broadcast_in_dim.52
  267.6 2.4 fusion.11
  270.1 3.2 %fusion.8 = bf16[4,32,896]{2,1,0:T(8,128)(2,1)S(1)} fusion(bf16[1536,1792]{1,0:T(8,128)(2,1)} %get-tuple-element.12, pred[4,32,1536]{2,1,0:T(32,128)(4,1)S(1)} %compare_and_fusion, f32[4,32,1536]{2,1,0:T(8,128)S(1)} %copy-done.3), kind=kOutput, calls=%fused_computation.8 | convolution fusion | flops 2114240512 | bytes 3964928 | tf_op jit(solution)/shard_map/dot_general | solution.py:43
  273.3 0.8 pad_maximum_fusion
  274.1 4.8 %all-to-all-start = ((bf16[4,32,1792]{2,1,0:T(8,128)(2,1)}), bf16[4,32,1792]{2,1,0:T(8,128)(2,1)S(1)}, u32[]{:S(2)}, u32[]{:S(2)}) async-start(bf16[4,32,1792]{2,1,0:T(8,128)(2,1)} %pad_maximum_fusion), calls=%async_computation | async-start | bytes 917504 | tf_op jit(solution)/shard_map/all_to_all | solution.py:50
  279.5 0.7 reduce
  280.5 0.7 copy.53
  281.2 4.0 %all-to-all-done = bf16[4,32,1792]{2,1,0:T(8,128)(2,1)S(1)} async-done(((bf16[4,32,1792]{2,1,0:T(8,128)(2,1)}), bf16[4,32,1792]{2,1,0:T(8,128)(2,1)S(1)}, u32[]{:S(2)}, u32[]{:S(2)}) %all-to-all-start) | async-done | bytes 458784 | tf_op jit(solution)/shard_map/all_to_all | solution.py:50
  285.3 0.7 copy.58
  286.0 0.7 copy.59
  286.7 1.2 copy.69
  287.9 1.2 copy.70
  289.1 0.9 copy-done
  290.1 1.2 copy.71
  (35 shorter events, 3.6 us)
Async XLA Ops:
  256.2 18.0 %all-to-all-start.1 = ((f32[4,1,1024]{2,1,0:T(1,128)}), f32[4,1,1024]{2,1,0:T(1,128)S(1)}, u32[]{:S(2)}, u32[]{:S(2)}) async-start(f32[4,1,1024]{2,1,0:T(1,128)} %reshape.158), calls=%async_computation.1 | async-start | bytes 32768 | tf_op jit(solution)/shard_map/all_to_all | solution.py:51
  267.5 2.6 copy-start.3
  273.3 13.4 %copy-start.2 = (bf16[896,1024]{1,0:T(8,128)(2,1)S(1)}, bf16[896,1024]{1,0:T(8,128)(2,1)}, u32[]{:S(2)}) copy-start(bf16[896,1024]{1,0:T(8,128)(2,1)} %get-tuple-element.13) | copy-start | bytes 5505028
  274.1 11.1 %all-to-all-start = ((bf16[4,32,1792]{2,1,0:T(8,128)(2,1)}), bf16[4,32,1792]{2,1,0:T(8,128)(2,1)S(1)}, u32[]{:S(2)}, u32[]{:S(2)}) async-start(bf16[4,32,1792]{2,1,0:T(8,128)(2,1)} %pad_maximum_fusion), calls=%async_computation | async-start | bytes 917504 | tf_op jit(solution)/shard_map/all_to_all | solution.py:50
  285.2 2.7 copy-start.1
  287.9 2.2 copy-start

commit v4 on v3

v4 whole, which is shorter than its diff:
```python
import jax
import jax.numpy as jnp
from jax import lax
from jax.experimental import pallas as pl
from jax.experimental.pallas import tpu as pltpu
from jax.sharding import PartitionSpec as P

BF = jnp.bfloat16
F32 = jnp.float32
LANES = 128
SIDE = 4
GROUP = 8
CHUNKS = ((0, 4), (8, 8), (24, 8), (16, 8), (4, 4))
MESH = pl.DeviceIdType.MESH


def dot32(a, b, dims, precision=None):
    return lax.dot_general(a, b, (dims, ((), ())), precision=precision, preferred_element_type=F32)


def moe_kernel(
    tok_ref, grad_ref, ids_ref, wts_ref, gate_ref, up_ref, down_ref,
    mixed_out, tgrad_out, route_out, gate_out, up_out, down_out, back_ref, whole_ref,
    tab_s, mine, blk, x_s, xt_s, g_s, hid_t, part, own, in_half, in_full, terms, rows_out, stage_a, stage_b,
    bk, mixed_acc, tgrad_acc, route_acc, final_v, route_in,
    ring_send, ring_recv, ret_send, ret_recv, a2a_send, a2a_recv, ag_send, ag_recv,
    pair_send, pair_recv, local_sem, stage_sem, fin_send, fin_recv,
):
    n_dp = lax.axis_size("dp")
    experts = lax.axis_size("expert")
    d = lax.axis_index("dp")
    e = lax.axis_index("expert")
    y = e // (2 * SIDE)
    z = (e // 2) % SIDE
    c = e % 2
    tok_rows, top = ids_ref.shape
    toks = n_dp * tok_rows
    tok_bits = tok_rows.bit_length() - 1
    slots_dp = rows_out.shape[0] // experts
    slots = slots_dp // n_dp
    quarter = own.shape[2]
    width = gate_ref.shape[0]
    to = ((d + n_dp - 1) % n_dp, (d + 1) % n_dp)

    barrier = pltpu.get_barrier_semaphore()
    for m in range(1, n_dp):
        pl.semaphore_signal(barrier, inc=1, device_id={"dp": (d + m) % n_dp}, device_id_type=MESH)

    def greet(step, carry):
        pl.semaphore_signal(
            barrier, inc=1, device_id={"expert": (e + step) % experts}, device_id_type=MESH
        )
        return carry

    lax.fori_loop(1, experts, greet, 0)

    def make_table():
        lane = lax.broadcasted_iota(jnp.int32, (tok_rows, LANES), 1)
        name = lane & (experts - 1)
        kind = lax.shift_right_logical(lane, experts.bit_length() - 1)
        chosen = jnp.zeros((tok_rows, LANES), F32)
        weight = jnp.zeros((tok_rows, LANES), F32)
        for k in range(top):
            same = ids_ref[:, k : k + 1] == name
            chosen += jnp.where(same, 1.0, 0.0)
            weight += jnp.where(same, wts_ref[:, k : k + 1], 0.0)
        row = lax.broadcasted_iota(jnp.int32, (tok_rows, tok_rows), 0)
        col = lax.broadcasted_iota(jnp.int32, (tok_rows, tok_rows), 1)
        below = jnp.where(row >= col, 1.0, 0.0).astype(BF)
        place = jnp.dot(below, chosen.astype(BF), preferred_element_type=F32) * chosen
        high = weight.astype(BF).astype(F32)
        middle = (weight - high).astype(BF).astype(F32)
        low = weight - high - middle
        value = jnp.where(kind == 0, place, jnp.where(kind == 1, high, jnp.where(kind == 2, middle, low)))
        tab_s[...] = value.astype(BF)

    make_table()
    pl.semaphore_wait(barrier, experts + n_dp - 2)

    sends = []

    def launch(item):
        item.start()
        sends.append(item)

    def block(p, h=None):
        if h is None:
            return whole_ref.at[pl.ds(p * toks, toks), :]
        rows = toks // 2
        return whole_ref.at[pl.ds(p * toks + h * rows, rows), :]

    def own_slice(src, number):
        rows = pl.ds(pl.multiple_of(src * tok_rows, tok_rows), tok_rows)
        return whole_ref.at[rows, pl.ds(number * width, LANES if number == 2 else width)]

    def to_slice(m, number):
        q = (d + m) % n_dp
        cols = pl.ds(pl.multiple_of(q * width, LANES), width)
        source = tab_s if number == 2 else (tok_ref, grad_ref)[number].at[:, cols]
        target = own_slice(d, number)
        if m == 0:
            return pltpu.make_async_copy(source, target, local_sem.at[number])
        return pltpu.make_async_remote_copy(
            src_ref=source, dst_ref=target, send_sem=a2a_send.at[m - 1, number],
            recv_sem=a2a_recv.at[m - 1, number], device_id={"dp": q}, device_id_type=MESH,
        )

    def from_slice(m, number):
        ref = own_slice((d + n_dp - m) % n_dp, number)
        return pltpu.make_async_remote_copy(
            src_ref=ref, dst_ref=ref, send_sem=a2a_send.at[m - 1, number],
            recv_sem=a2a_recv.at[m - 1, number], device_id={"dp": (d + m) % n_dp}, device_id_type=MESH,
        )

    def spot(da, db, rel):
        return db * GROUP + rel * SIDE + da

    def ag_copy_to(axis, way, da, db, h):
        step = SIDE - 1 if way == 0 else 1
        seen = 1 if way == 0 else SIDE - 1
        da2 = (da + seen) % SIDE if axis == 0 else da
        db2 = (db + seen) % SIDE if axis == 1 else db
        along_y = 1 - c if axis == 0 else c
        y2 = (y + step * along_y) % SIDE
        z2 = (z + step * (1 - along_y)) % SIDE
        return pltpu.make_async_remote_copy(
            src_ref=block(spot(da, db, 0), h),
            dst_ref=block(spot(da2, db2, 0), h),
            send_sem=ag_send.at[da * SIDE + db, axis * 2 + way, h],
            recv_sem=ag_recv.at[da2 * SIDE + db2, h],
            device_id={"expert": (y2 * SIDE + z2) * 2 + c},
            device_id_type=MESH,
        )

    def ag_wait(da, db, h):
        ref = block(spot(da, db, 0), h)
        pltpu.make_async_remote_copy(
            src_ref=ref, dst_ref=ref, send_sem=ag_send.at[0, 0, 0], recv_sem=ag_recv.at[da * SIDE + db, h],
            device_id={"expert": (e + 1) % experts}, device_id_type=MESH,
        ).wait_recv()

    def pair_copy(da, db):
        return pltpu.make_async_remote_copy(
            src_ref=block(spot(da, db, 0)), dst_ref=block(spot(da, db, 1)),
            send_sem=pair_send.at[da * SIDE + db], recv_sem=pair_recv.at[da * SIDE + db],
            device_id={"expert": e + 1 - 2 * c}, device_id_type=MESH,
        )

    def spread(axis, da, db):
        for way, h in ((0, 0), (1, 1), (0, 1), (1, 0)):
            launch(ag_copy_to(axis, way, da, db, h))

    def slices():
        for m in (1, 3, 2, 0):
            for number in range(3):
                to_slice(m, number).start()
        for number in range(3):
            to_slice(0, number).wait()
            for m in range(1, n_dp):
                from_slice(m, number).wait_recv()

    def mine_copy():
        return pltpu.make_async_copy(block(0), mine, local_sem.at[5])

    def first_phase():
        spread(0, 0, 0)
        launch(pair_copy(0, 0))
        mine_copy().start()
        ag_wait(1, 0, 0)
        launch(ag_copy_to(0, 0, 1, 0, 0))
        ag_wait(3, 0, 1)
        launch(ag_copy_to(0, 1, 3, 0, 1))
        spread(1, 0, 0)
        for da in (1, 3):
            ag_wait(da, 0, 1 if da == 1 else 0)
            launch(pair_copy(da, 0))
            spread(1, da, 0)
        ag_wait(2, 0, 0)
        ag_wait(2, 0, 1)
        launch(pair_copy(2, 0))
        spread(1, 2, 0)
        mine_copy().wait()

    def second_phase(da):
        ag_wait(da, 1, 0)
        launch(ag_copy_to(1, 0, da, 1, 0))
        ag_wait(da, 3, 1)
        launch(ag_copy_to(1, 1, da, 3, 1))
        ag_wait(da, 1, 1)
        launch(pair_copy(da, 1))
        ag_wait(da, 3, 0)
        launch(pair_copy(da, 3))

    def third_phase(da):
        ag_wait(da, 2, 0)
        ag_wait(da, 2, 1)
        launch(pair_copy(da, 2))

    def size_of(k):
        return CHUNKS[k][1] * slots_dp

    def rows_of(k, part_half=None):
        start = CHUNKS[k][0] * slots_dp
        if part_half is None:
            return pl.ds(start, size_of(k))
        return pl.ds(start + part_half * (size_of(k) // 2), size_of(k) // 2)

    def half_rows(k):
        return pl.ds(CHUNKS[k][0] * slots_dp // 2, size_of(k) // 2)

    def cols_of(q):
        return pl.ds(pl.multiple_of(q * quarter, quarter), quarter)

    def take_chunk(k):
        first, count = CHUNKS[k]
        for p in range(first, first + count):
            if (p // SIDE) % 2 == 1:
                pair_copy(p % SIDE, p // GROUP).wait_recv()
        load = pltpu.make_async_copy(
            whole_ref.at[pl.ds(first * toks, count * toks), :], blk.at[pl.ds(0, count * toks), :], local_sem.at[3]
        )
        load.start()
        load.wait()
        pair_rows = 2 * slots_dp
        pair_toks = 2 * toks

        def one(i, carry):
            span = pl.ds(pl.multiple_of(i * pair_toks, pair_toks), pair_toks)
            line = lax.broadcasted_iota(jnp.int32, (16, LANES), 0)
            lane = lax.broadcasted_iota(jnp.int32, (16, LANES), 1)
            want = jnp.where((lane == line * experts + e) & (line < 4), 1.0, 0.0).astype(BF)
            found = dot32(want, blk[span, 2 * width :], ((1,), (1,)))
            place = found[0:1, :]
            scale = found[1:2, :] + found[2:3, :] + found[3:4, :]
            token = lax.broadcasted_iota(jnp.int32, (1, pair_toks), 1)
            base = (lax.shift_right_logical(token, tok_bits) * slots).astype(F32)
            goal = jnp.where(place > 0.0, base + place - 1.0, -1.0)
            row = lax.broadcasted_iota(jnp.int32, (pair_rows, pair_toks), 0).astype(F32)
            hit = row == goal
            picked = jnp.dot(
                jnp.where(hit, 1.0, 0.0).astype(BF), blk[span, : 2 * width], preferred_element_type=F32
            )
            scales = jnp.sum(jnp.where(hit, scale, 0.0), axis=1, keepdims=True)
            x_s[pl.ds(pl.multiple_of(i * pair_rows, pair_rows), pair_rows), :] = picked[:, :width].astype(BF)
            g_s[pl.ds(pl.multiple_of(first * slots_dp + i * pair_rows, pair_rows), pair_rows), :] = (
                picked[:, width:] * scales
            ).astype(BF)
            return carry

        lax.fori_loop(0, count // 2, one, 0)

    def copy(k, way, number, source, target):
        return pltpu.make_async_remote_copy(
            src_ref=source, dst_ref=target, send_sem=ring_send.at[k, way, number],
            recv_sem=ring_recv.at[k, way, number], device_id={"dp": to[way]}, device_id_type=MESH,
        )

    def toward(way):
        return part.at[2 if way == 0 else 0]

    def rs_copy(k, way, number):
        if number == 0:
            return copy(k, way, 0, part.at[1, :, rows_of(k, way), :], in_half.at[way, :, half_rows(k), :])
        h = way if number == 2 else 1 - way
        return copy(
            k, way, number, toward(way).at[:, rows_of(k, h), :], in_full.at[way, :, rows_of(k, h), :]
        )

    def ag_terms(k, way, number, q):
        h = way if number in (3, 5) else 1 - way
        ref = terms.at[:, rows_of(k, h), cols_of(q)]
        return copy(k, way, number, ref, ref)

    def ring_copy(k, way, number):
        return ag_terms(k, way, number, to[1 - way] if number == 5 else d)

    def ring_arrival(k, way, number):
        return ag_terms(k, way, number, (d + 2) % n_dp if number == 5 else to[1 - way])

    def partial(k, q, i):
        if i == 2:
            return dot32(g_s[rows_of(k), :], down_ref[cols_of(q), :], ((1,), (1,)))
        right = (gate_ref, up_ref)[i]
        return jnp.dot(x_s[pl.ds(0, size_of(k)), :], right[:, cols_of(q)], preferred_element_type=F32)

    def stage0(k):
        def one(step, carry):
            m = (step + 1) % (n_dp - 1)
            q = (d + m + 1) % n_dp
            for i in range(3):
                part[m, i, rows_of(k), :] = partial(k, q, i).astype(BF)
            return carry

        lax.fori_loop(0, n_dp - 1, one, 0)
        for number in range(2):
            for way in range(2):
                rs_copy(k, way, number).start()
        for i in range(3):
            own[i, rows_of(k), :] = partial(k, d, i)
        xt_s[:, rows_of(k)] = x_s[pl.ds(0, size_of(k)), :].T

    def stage1(k):
        for way in range(2):
            rs_copy(k, way, 0).wait_recv()
            m = 2 if way == 0 else 0
            for i in range(3):
                span = rows_of(k, way)
                total = part[m, i, span, :].astype(F32) + in_half[way, i, half_rows(k), :].astype(F32)
                part[m, i, span, :] = total.astype(BF)
            rs_copy(k, way, 2).start()

    def stage2(k):
        for number in (1, 2):
            for way in range(2):
                rs_copy(k, way, number).wait_recv()

        def total(i, span):
            return own[i, span, :] + in_full[0, i, span, :].astype(F32) + in_full[1, i, span, :].astype(F32)

        step_rows = 2 * slots_dp

        def act(step, carry):
            start = CHUNKS[k][0] * slots_dp + step * step_rows
            span = pl.ds(pl.multiple_of(start, step_rows), step_rows)
            gate = total(0, span)
            up = total(1, span)
            hgrad = total(2, span)
            sig = jax.nn.sigmoid(gate)
            val = gate * sig
            slope = sig * (1.0 + gate * (1.0 - sig))
            terms[0, span, cols_of(d)] = (val * up).astype(BF)
            terms[1, span, cols_of(d)] = (hgrad * up * slope).astype(BF)
            terms[2, span, cols_of(d)] = (hgrad * val).astype(BF)
            return carry

        lax.fori_loop(0, size_of(k) // step_rows, act, 0)
        for number in (3, 4):
            for way in range(2):
                ring_copy(k, way, number).start()

    def stage3(k):
        for way in range(2):
            ring_arrival(k, way, 3).wait_recv()
            ring_copy(k, way, 5).start()

    def home(p):
        return pl.ds(pl.multiple_of(p * slots_dp, slots_dp), slots_dp)

    def back_copy(k, i):
        db = CHUNKS[k][0] // GROUP
        p = CHUNKS[k][0] + i
        s = (c + p // SIDE) % 2
        da = p % SIDE
        y2 = (y + da * (1 - s) + db * s) % SIDE
        z2 = (z + db * (1 - s) + da * s) % SIDE
        return pltpu.make_async_remote_copy(
            src_ref=rows_out.at[home(p), :],
            dst_ref=back_ref.at[home(p), :],
            send_sem=ret_send.at[p],
            recv_sem=ret_recv.at[p],
            device_id={"expert": (y2 * SIDE + z2) * 2 + s},
            device_id_type=MESH,
        )

    def self_copy():
        return pltpu.make_async_copy(rows_out.at[home(0), :], back_ref.at[home(0), :], local_sem.at[4])

    def each_back(k, act):
        def one(i, carry):
            act(back_copy(k, i))
            return carry

        lax.fori_loop(1 if k == 0 else 0, CHUNKS[k][1], one, 0)

    def stage4(k):
        for number in (4, 5):
            for way in range(2):
                ring_arrival(k, way, number).wait_recv()
        half = size_of(k) // 2

        def one(h, carry):
            span = pl.ds(pl.multiple_of(CHUNKS[k][0] * slots_dp + h * half, half), half)
            rows_out[span, :width] = jnp.dot(
                terms[0, span, :], down_ref[...], preferred_element_type=F32
            ).astype(BF)
            rows_out[span, width:] = (
                dot32(terms[1, span, :], gate_ref[...], ((1,), (1,)))
                + dot32(terms[2, span, :], up_ref[...], ((1,), (1,)))
            ).astype(BF)
            return carry

        lax.fori_loop(0, 2, one, 0)
        if k == 0:
            self_copy().start()
        each_back(k, lambda item: item.start())
        hid_t[:, rows_of(k)] = terms[0, rows_of(k), :].T

    def fold(k):
        first, count = CHUNKS[k]
        rows = size_of(k)
        each_back(k, lambda item: item.wait_recv())
        if k == 0:
            self_copy().wait()
        load = pltpu.make_async_copy(back_ref.at[rows_of(k), :], bk.at[pl.ds(0, rows), :], local_sem.at[6])
        load.start()
        row = lax.broadcasted_iota(jnp.int32, (1, rows), 1)
        index = lax.shift_right_logical(row * (65536 // slots_dp + 1), 16)
        local = (row - index * slots_dp).astype(F32)
        p = first + index
        db = first // GROUP
        da = p & (SIDE - 1)
        core = (c + lax.shift_right_logical(p, 2)) & 1
        y2 = (y + 2 * SIDE - (da * (1 - c) + db * c)) & (SIDE - 1)
        z2 = (z + 2 * SIDE - (db * (1 - c) + da * c)) & (SIDE - 1)
        sender = (y2 * SIDE + z2) * 2 + core
        lane = lax.broadcasted_iota(jnp.int32, (LANES, rows), 0)
        names = [jnp.where(lane == kind * experts + sender, 1.0, 0.0) for kind in range(4)]
        table = mine[:, 2 * width :]
        found = [jnp.dot(table, name.astype(BF), preferred_element_type=F32) for name in names]
        token = lax.broadcasted_iota(jnp.int32, (toks, rows), 0)
        base = (lax.shift_right_logical(token, tok_bits) * slots).astype(F32)
        hit = (found[0] > 0.0) & (local == base + found[0] - 1.0)
        scaled = jnp.concatenate([jnp.where(hit, found[i], 0.0).astype(BF) for i in (1, 2, 3)], axis=0)
        once = jnp.where(hit, 1.0, 0.0).astype(BF)
        load.wait()
        outs = bk[pl.ds(0, rows), :width]
        three = jnp.dot(scaled, outs, preferred_element_type=F32)
        mixed = three[:toks] + three[toks : 2 * toks] + three[2 * toks :]
        tgrad = jnp.dot(once, bk[pl.ds(0, rows), width:], preferred_element_type=F32)
        dots = dot32(mine[:, width : 2 * width], outs, ((1,), (1,)))
        route = dot32(jnp.where(hit, dots, 0.0), names[0], ((1,), (1,)), lax.Precision.HIGHEST)
        if k == 0:
            mixed_acc[...] = mixed
            tgrad_acc[...] = tgrad
            route_acc[...] = route
        else:
            mixed_acc[...] += mixed
            tgrad_acc[...] += tgrad
            route_acc[...] += route

    def weight_grads():
        span = stage_a.shape[2]
        tall = stage_b.shape[1]

        def out_copy(kind, i, slot):
            if kind == 2:
                target = down_out.at[pl.ds(pl.multiple_of(i * tall, tall), tall), :]
                return pltpu.make_async_copy(stage_b.at[slot], target, stage_sem.at[kind, slot])
            target = (gate_out, up_out)[kind].at[:, pl.ds(pl.multiple_of(i * span, span), span)]
            return pltpu.make_async_copy(stage_a.at[slot], target, stage_sem.at[kind, slot])

        for kind in range(3):
            count = gate_ref.shape[1] // (tall if kind == 2 else span)

            def one(i, carry, kind=kind):
                slot = i % 2

                @pl.when(i >= 2)
                def _():
                    out_copy(kind, i - 2, slot).wait()

                if kind == 2:
                    left = hid_t[pl.ds(pl.multiple_of(i * tall, tall), tall), :]
                    stage_b[slot] = jnp.dot(left, g_s[...], preferred_element_type=F32).astype(BF)
                else:
                    right = terms[1 + kind, :, pl.ds(pl.multiple_of(i * span, span), span)]
                    stage_a[slot] = jnp.dot(xt_s[...], right, preferred_element_type=F32).astype(BF)
                out_copy(kind, i, slot).start()
                return carry

            lax.fori_loop(0, count, one, 0)
            out_copy(kind, count - 2, count % 2).wait()
            out_copy(kind, count - 1, (count - 1) % 2).wait()

    def final_copy(m, number):
        q = (d + m) % n_dp
        rows = pl.ds(pl.multiple_of(q * tok_rows, tok_rows), tok_rows)
        if number == 2:
            source, target = route_acc.at[rows, :], route_in.at[d]
        else:
            source = final_v.at[rows, pl.ds(number * width, width)]
            target = (mixed_out, tgrad_out)[number].at[:, pl.ds(pl.multiple_of(d * width, LANES), width)]
        if m == 0:
            return pltpu.make_async_copy(source, target, fin_send.at[m, number])
        return pltpu.make_async_remote_copy(
            src_ref=source, dst_ref=target, send_sem=fin_send.at[m, number],
            recv_sem=fin_recv.at[m - 1, number], device_id={"dp": q}, device_id_type=MESH,
        )

    def final_arrival(m, number):
        src = (d + n_dp - m) % n_dp
        if number == 2:
            ref = route_in.at[src]
        else:
            ref = (mixed_out, tgrad_out)[number].at[:, pl.ds(pl.multiple_of(src * width, LANES), width)]
        return pltpu.make_async_remote_copy(
            src_ref=ref, dst_ref=ref, send_sem=fin_send.at[m, number],
            recv_sem=fin_recv.at[m - 1, number], device_id={"dp": (d + m) % n_dp}, device_id_type=MESH,
        )

    def finish():
        final_v[:, :width] = mixed_acc[...].astype(BF)
        final_v[:, width:] = tgrad_acc[...].astype(BF)
        for m in (2, 1, 3, 0):
            for number in range(3):
                final_copy(m, number).start()
        for number in (2, 0, 1):
            final_copy(0, number).wait()
            for m in range(1, n_dp):
                final_arrival(m, number).wait_recv()
        total = route_in[0]
        for q in range(1, n_dp):
            total = total + route_in[q]
        lane = lax.broadcasted_iota(jnp.int32, (tok_rows, LANES), 1)
        place = lax.broadcasted_iota(jnp.int32, (tok_rows, top), 1)
        result = jnp.zeros((tok_rows, top), F32)
        for k in range(top):
            col = jnp.sum(jnp.where(lane == ids_ref[:, k : k + 1], total, 0.0), axis=1, keepdims=True)
            result = jnp.where(place == k, col, result)
        route_out[...] = result

    slices()
    first_phase()
    last = len(CHUNKS)
    for t in range(last + 4):
        if 0 <= t - 1 < last:
            stage1(t - 1)
        if t == 1:
            second_phase(3)
            second_phase(2)
        if 0 <= t - 2 < last:
            stage2(t - 2)
        if 0 <= t - 3 < last:
            stage3(t - 3)
        if t == 2:
            for da in (0, 1, 3, 2):
                third_phase(da)
        if t < last:
            take_chunk(t)
            stage0(t)
        if t == 0:
            second_phase(0)
            second_phase(1)
        if 0 <= t - 4 < last:
            stage4(t - 4)
        if 0 <= t - 6 < last:
            fold(t - 6)
    weight_grads()
    for k in range(last - 2, last):
        fold(k)
    finish()

    for m in range(1, n_dp):
        for number in range(3):
            to_slice(m, number).wait_send()
            final_copy(m, number).wait_send()
    for item in sends:
        item.wait_send()
    for k in range(last):
        for way in range(2):
            for number in range(3):
                rs_copy(k, way, number).wait_send()
                ring_copy(k, way, number + 3).wait_send()
        each_back(k, lambda item: item.wait_send())


def moe(tokens, out_grad, ids, weights, gate, up, down, experts, n_dp):
    width, hidden = gate.shape
    tok_rows, top = ids.shape
    slots = min(tok_rows, 3 * tok_rows * top // (2 * experts))
    toks = n_dp * tok_rows
    slots_dp = n_dp * slots
    rows = experts * slots_dp
    quarter = hidden // n_dp
    chunk = GROUP * slots_dp
    both = 2 * width
    last = len(CHUNKS)
    dma = pltpu.SemaphoreType.DMA
    vmem = pltpu.VMEM
    anywhere = pl.BlockSpec(memory_space=pl.ANY)
    inside = pl.BlockSpec(memory_space=pltpu.VMEM)
    return pl.pallas_call(
        moe_kernel,
        out_shape=(
            jax.ShapeDtypeStruct(tokens.shape, BF),
            jax.ShapeDtypeStruct(tokens.shape, BF),
            jax.ShapeDtypeStruct(ids.shape, F32),
            jax.ShapeDtypeStruct((width, hidden), BF),
            jax.ShapeDtypeStruct((width, hidden), BF),
            jax.ShapeDtypeStruct((hidden, width), BF),
            jax.ShapeDtypeStruct((rows, both), BF),
            jax.ShapeDtypeStruct((experts * toks, both + LANES), BF),
        ),
        in_specs=[inside] * 7,
        out_specs=(anywhere, anywhere, inside) + (anywhere,) * 5,
        scratch_shapes=[
            vmem((tok_rows, LANES), BF),
            vmem((toks, both + LANES), BF),
            vmem((GROUP * toks, both + LANES), BF),
            vmem((chunk, width), BF),
            vmem((width, rows), BF),
            vmem((rows, width), BF),
            vmem((hidden, rows), BF),
            vmem((n_dp - 1, 3, rows, quarter), BF),
            vmem((3, rows, quarter), F32),
            vmem((2, 3, rows // 2, quarter), BF),
            vmem((2, 3, rows, quarter), BF),
            vmem((3, rows, hidden), BF),
            vmem((rows, both), BF),
            vmem((2, width, quarter), BF),
            vmem((2, quarter, width), BF),
            vmem((chunk, both), BF),
            vmem((toks, width), F32),
            vmem((toks, width), F32),
            vmem((toks, LANES), F32),
            vmem((toks, both), BF),
            vmem((n_dp, tok_rows, LANES), F32),
            dma((last, 2, 6)),
            dma((last, 2, 6)),
            dma((experts,)),
            dma((experts,)),
            dma((n_dp - 1, 3)),
            dma((n_dp - 1, 3)),
            dma((SIDE * SIDE, 4, 2)),
            dma((SIDE * SIDE, 2)),
            dma((SIDE * SIDE,)),
            dma((SIDE * SIDE,)),
            dma((7,)),
            dma((3, 2)),
            dma((n_dp, 3)),
            dma((n_dp - 1, 3)),
        ],
        compiler_params=pltpu.CompilerParams(
            collective_id=0, has_side_effects=True, vmem_limit_bytes=67043328
        ),
    )(tokens, out_grad, ids, weights, gate, up, down)


def per_device(tokens, ids, weights, out_grad, gate_weight, up_weight, down_weight):
    experts = lax.axis_size("expert")
    n_dp = lax.axis_size("dp")
    mixed, tgrad, route, gate_grad, up_grad, down_grad, _, _ = moe(
        tokens, out_grad, ids, weights, gate_weight[0], up_weight[0], down_weight[0], experts, n_dp
    )
    return (mixed, tgrad, route, gate_grad[None], up_grad[None], down_grad[None])


def solution(mesh):
    rows = P(("dp", "expert"), None)
    weights = (P("expert", "dp", None), P("expert", "dp", None), P("expert", None, "dp"))
    return jax.shard_map(
        per_device,
        mesh=mesh,
        in_specs=(rows, rows, rows, rows) + weights,
        out_specs=(rows, rows, rows) + weights,
        check_vma=False,
    )
```

time: 297 us -> 281 us (0.946)
  Pallas kernels: 248 us -> 262 us
  starting transfers between devices: 8.91 us -> 0 us
  matrix products: 8.48 us -> 0 us
  other arithmetic: 4.12 us -> 0 us
  waiting for transfers between devices: 4.05 us -> 0 us
  local copies, waits for them, and re-layouts: 17 us -> 13.8 us
    pallas_call x1, Pallas kernels: 248 us -> 262 us  [moe(): pl.pallas_call(moe_kernel, out_shape=(jax.ShapeDtypeStruct(tokens.shape,...]
    all_to_all x2 -> x0, starting transfers between devices: 8.91 us -> none  [the longest x1 4.8 us: combine(): both = lax.all_to_all(both, 'dp', 0, 0, tiled=True)]
    dot_general x3 -> x0, matrix products: 8.48 us -> none  [the longest x2 5.25 us: dot32(): return lax.dot_general(a, b, (dims, ((), ())), preferred_element_type=F32)]
    unnamed x18 -> x12, local copies, waits for them, and re-layouts: 7.76 us -> 13.8 us
    all_to_all x2 -> x0, waiting for transfers between devices: 4.05 us -> none  [the longest x1 4.04 us: combine(): both = lax.all_to_all(both, 'dp', 0, 0, tiled=True)]
    broadcast_in_dim x2 -> x0, local copies, waits for them, and re-layouts: 3.26 us -> none  [combine(): scaled = jnp.where(hit, weight[:, :, None], 0.0).reshape(toks, -1)]
  transfers between devices with their start and end apart: 2 -> 0, of which waited for: 1 -> 0; matrix products, arithmetic and copies ran while one was open for 5% -> 0% of each run, Pallas kernels for 0% -> 0%
where the time goes in v4:
time: 281 us; the launch traced here: 276 us
  Pallas kernels  262 us (93%)
  local copies, waits for them, and re-layouts  13.8 us (5%)
    pallas_call x1, Pallas kernels, moe(): pl.pallas_call(moe_kernel, out_shape=(jax.ShapeDtypeStruct(tokens.shape,...  262 us
    unnamed x12, local copies, waits for them, and re-layouts  13.8 us

profile of v4, /device:TPU:34, one launch (start us, length us, event | category | flops | bytes accessed | tf_op | source)
XLA Modules:
  0.0 276.2 jit_solution(4085989408432773950)
XLA Ops:
  0.6 1.4 copy.13.ids_ref
  2.0 1.4 copy.14.wts_ref
  3.4 261.8 %shard_map.118 = (bf16[32,3584]{1,0:T(8,128)(2,1)}, bf16[32,3584]{1,0:T(8,128)(2,1)}, f32[32,8]{1,0:T(8,128)}, bf16[896,1024]{1,0:T(8,128)(2,1)}, bf16[896,1024]...) custom-call(bf16[32,3584]{1,0:T(8,128)(2,1)} %tok_ref.1, ...), custom_call_target="tpu_custom_call" | custom-call | tf_op jit(solution)/shard_map/pallas_call | solution.py:582
  265.2 1.4 copy.15
  266.6 1.6 copy.21
  268.2 1.6 copy.22
  269.8 0.0 copy-start.1
  269.8 3.0 %copy.23 = bf16[1,896,1024]{2,1,0:T(8,128)(2,1)} copy(bf16[1,896,1024]{2,1,0:T(8,128)(2,1)} %bitcast.8) | data formatting | bytes 3670016
  272.8 0.0 copy-done.1
  272.8 0.0 copy-start
  272.8 1.2 copy.24
  274.1 0.9 copy-done
  275.0 1.2 copy.25
Async XLA Ops:
  269.8 3.0 %copy-start.1 = (bf16[896,1024]{1,0:T(8,128)(2,1)S(1)}, bf16[896,1024]{1,0:T(8,128)(2,1)}, u32[]{:S(2)}) copy-start(bf16[896,1024]{1,0:T(8,128)(2,1)} %get-tuple-element.16) | copy-start | bytes 5505028
  272.8 2.2 copy-start

commit v5 on v4

--- a/solution.py
+++ b/solution.py
@@ -21,7 +21,7 @@
 def moe_kernel(
     tok_ref, grad_ref, ids_ref, wts_ref, gate_ref, up_ref, down_ref,
     mixed_out, tgrad_out, route_out, gate_out, up_out, down_out, back_ref, whole_ref,
-    tab_s, mine, blk, x_s, xt_s, g_s, hid_t, part, own, in_half, in_full, terms, rows_out, stage_a, stage_b,
+    square, tab_s, mine, blk, x_s, xt_s, g_s, hid_t, part, own, in_half, in_full, terms, rows_out, stage_a, stage_b,
     bk, mixed_acc, tgrad_acc, route_acc, final_v, route_in,
     ring_send, ring_recv, ret_send, ret_recv, a2a_send, a2a_recv, ag_send, ag_recv,
     pair_send, pair_recv, local_sem, stage_sem, fin_send, fin_recv,
@@ -33,7 +33,7 @@
     y = e // (2 * SIDE)
     z = (e // 2) % SIDE
     c = e % 2
-    tok_rows, top = ids_ref.shape
+    top, tok_rows = ids_ref.shape
     toks = n_dp * tok_rows
     tok_bits = tok_rows.bit_length() - 1
     slots_dp = rows_out.shape[0] // experts
@@ -55,24 +55,27 @@
     lax.fori_loop(1, experts, greet, 0)
 
     def make_table():
-        lane = lax.broadcasted_iota(jnp.int32, (tok_rows, LANES), 1)
-        name = lane & (experts - 1)
-        kind = lax.shift_right_logical(lane, experts.bit_length() - 1)
-        chosen = jnp.zeros((tok_rows, LANES), F32)
-        weight = jnp.zeros((tok_rows, LANES), F32)
+        line = lax.broadcasted_iota(jnp.int32, (LANES, tok_rows), 0)
+        name = line & (experts - 1)
+        kind = lax.shift_right_logical(line, experts.bit_length() - 1)
+        chosen = jnp.zeros((LANES, tok_rows), F32)
+        weight = jnp.zeros((LANES, tok_rows), F32)
         for k in range(top):
-            same = ids_ref[:, k : k + 1] == name
+            same = ids_ref[k : k + 1, :] == name
             chosen += jnp.where(same, 1.0, 0.0)
-            weight += jnp.where(same, wts_ref[:, k : k + 1], 0.0)
+            weight += jnp.where(same, wts_ref[k : k + 1, :], 0.0)
         row = lax.broadcasted_iota(jnp.int32, (tok_rows, tok_rows), 0)
         col = lax.broadcasted_iota(jnp.int32, (tok_rows, tok_rows), 1)
-        below = jnp.where(row >= col, 1.0, 0.0).astype(BF)
-        place = jnp.dot(below, chosen.astype(BF), preferred_element_type=F32) * chosen
+        before = jnp.where(row <= col, 1.0, 0.0).astype(BF)
+        place = jnp.dot(chosen.astype(BF), before, preferred_element_type=F32) * chosen
         high = weight.astype(BF).astype(F32)
         middle = (weight - high).astype(BF).astype(F32)
         low = weight - high - middle
-        value = jnp.where(kind == 0, place, jnp.where(kind == 1, high, jnp.where(kind == 2, middle, low)))
-        tab_s[...] = value.astype(BF)
+        square[...] = jnp.zeros_like(square)
+        square[:, :tok_rows] = jnp.where(
+            kind == 0, place, jnp.where(kind == 1, high, jnp.where(kind == 2, middle, low))
+        )
+        tab_s[...] = square[...].T[:tok_rows].astype(BF)
 
     make_table()
     pl.semaphore_wait(barrier, experts + n_dp - 2)
@@ -511,43 +514,49 @@
         total = route_in[0]
         for q in range(1, n_dp):
             total = total + route_in[q]
-        lane = lax.broadcasted_iota(jnp.int32, (tok_rows, LANES), 1)
-        place = lax.broadcasted_iota(jnp.int32, (tok_rows, top), 1)
-        result = jnp.zeros((tok_rows, top), F32)
+        square[:tok_rows, :] = total
+        turned = square[...].T[:, :tok_rows]
+        line = lax.broadcasted_iota(jnp.int32, (LANES, tok_rows), 0)
+        place = lax.broadcasted_iota(jnp.int32, (top, tok_rows), 0)
+        result = jnp.zeros((top, tok_rows), F32)
         for k in range(top):
-            col = jnp.sum(jnp.where(lane == ids_ref[:, k : k + 1], total, 0.0), axis=1, keepdims=True)
-            result = jnp.where(place == k, col, result)
+            row = jnp.sum(jnp.where(line == ids_ref[k : k + 1, :], turned, 0.0), axis=0, keepdims=True)
+            result = jnp.where(place == k, row, result)
         route_out[...] = result
 
     slices()
     first_phase()
     last = len(CHUNKS)
-    for t in range(last + 4):
-        if 0 <= t - 1 < last:
-            stage1(t - 1)
-        if t == 1:
+    take_chunk(0)
+    stage0(0)
+    second_phase(0)
+    second_phase(1)
+    for k in range(last + 1):
+        if k < last:
+            stage1(k)
+        if k >= 1:
+            stage3(k - 1)
+        if k == 0:
             second_phase(3)
             second_phase(2)
-        if 0 <= t - 2 < last:
-            stage2(t - 2)
-        if 0 <= t - 3 < last:
-            stage3(t - 3)
-        if t == 2:
+            stage2(0)
+        if k + 1 < last:
+            take_chunk(k + 1)
+            stage0(k + 1)
+        if 1 <= k < last:
+            stage2(k)
+        if k == 1:
             for da in (0, 1, 3, 2):
                 third_phase(da)
-        if t < last:
-            take_chunk(t)
-            stage0(t)
-        if t == 0:
-            second_phase(0)
-            second_phase(1)
-        if 0 <= t - 4 < last:
-            stage4(t - 4)
-        if 0 <= t - 6 < last:
-            fold(t - 6)
+        if k == last:
+            fold(last - 3)
+        if k >= 1:
+            stage4(k - 1)
+        if 2 <= k <= last - 2:
+            fold(k - 2)
     weight_grads()
-    for k in range(last - 2, last):
-        fold(k)
+    fold(last - 2)
+    fold(last - 1)
     finish()
 
     for m in range(1, n_dp):
@@ -584,7 +593,7 @@
         out_shape=(
             jax.ShapeDtypeStruct(tokens.shape, BF),
             jax.ShapeDtypeStruct(tokens.shape, BF),
-            jax.ShapeDtypeStruct(ids.shape, F32),
+            jax.ShapeDtypeStruct((top, tok_rows), F32),
             jax.ShapeDtypeStruct((width, hidden), BF),
             jax.ShapeDtypeStruct((width, hidden), BF),
             jax.ShapeDtypeStruct((hidden, width), BF),
@@ -594,6 +603,7 @@
         in_specs=[inside] * 7,
         out_specs=(anywhere, anywhere, inside) + (anywhere,) * 5,
         scratch_shapes=[
+            vmem((LANES, LANES), F32),
             vmem((tok_rows, LANES), BF),
             vmem((toks, both + LANES), BF),
             vmem((GROUP * toks, both + LANES), BF),
@@ -633,7 +643,7 @@
         compiler_params=pltpu.CompilerParams(
             collective_id=0, has_side_effects=True, vmem_limit_bytes=67043328
         ),
-    )(tokens, out_grad, ids, weights, gate, up, down)
+    )(tokens, out_grad, ids.T, weights.T, gate, up, down)
 
 
 def per_device(tokens, ids, weights, out_grad, gate_weight, up_weight, down_weight):
@@ -642,7 +652,7 @@
     mixed, tgrad, route, gate_grad, up_grad, down_grad, _, _ = moe(
         tokens, out_grad, ids, weights, gate_weight[0], up_weight[0], down_weight[0], experts, n_dp
     )
-    return (mixed, tgrad, route, gate_grad[None], up_grad[None], down_grad[None])
+    return (mixed, tgrad, route.T, gate_grad[None], up_grad[None], down_grad[None])
 
 
 def solution(mesh):

time: 281 us -> 248 us (0.88)
  Pallas kernels: 262 us -> 233 us
  local copies, waits for them, and re-layouts: 13.8 us -> 10.9 us
    pallas_call x1, Pallas kernels: 262 us -> 233 us  [moe(): pl.pallas_call(moe_kernel, out_shape=(jax.ShapeDtypeStruct(tokens.shape,...]
    unnamed x12 -> x10, local copies, waits for them, and re-layouts: 13.8 us -> 10.9 us
where the time goes in v5:
time: 248 us; the launch traced here: 245 us
  Pallas kernels  233 us (94%)
  local copies, waits for them, and re-layouts  10.9 us (4%)
    pallas_call x1, Pallas kernels, moe(): pl.pallas_call(moe_kernel, out_shape=(jax.ShapeDtypeStruct(tokens.shape,...  233 us
    unnamed x10, local copies, waits for them, and re-layouts  10.9 us

profile of v5, /device:TPU:34, one launch (start us, length us, event | category | flops | bytes accessed | tf_op | source)
XLA Modules:
  0.0 245.0 jit_solution(5838891385297363407)
XLA Ops:
  0.6 233.4 %shard_map.118 = (bf16[32,3584]{1,0:T(8,128)(2,1)}, bf16[32,3584]{1,0:T(8,128)(2,1)}, f32[8,32]{1,0:T(8,128)}, bf16[896,1024]{1,0:T(8,128)(2,1)}, bf16[896,1024]...) custom-call(bf16[32,3584]{1,0:T(8,128)(2,1)} %tok_ref.1, ...), custom_call_target="tpu_custom_call" | custom-call | tf_op jit(solution)/shard_map/pallas_call | solution.py:591
  234.0 1.6 copy.19
  235.7 1.6 copy.20
  237.3 1.3 copy.21
  238.6 0.0 copy-start.1
  238.6 3.0 %copy.22 = bf16[1,896,1024]{2,1,0:T(8,128)(2,1)} copy(bf16[1,896,1024]{2,1,0:T(8,128)(2,1)} %bitcast.11) | data formatting | bytes 3670016
  241.6 0.0 copy-done.1
  241.6 0.0 copy-start
  241.6 1.2 copy.23
  242.8 0.9 copy-done
  243.7 1.2 copy.24
Async XLA Ops:
  238.6 3.0 %copy-start.1 = (bf16[896,1024]{1,0:T(8,128)(2,1)S(1)}, bf16[896,1024]{1,0:T(8,128)(2,1)}, u32[]{:S(2)}) copy-start(bf16[896,1024]{1,0:T(8,128)(2,1)} %get-tuple-element.16) | copy-start | bytes 5505028
  241.6 2.2 copy-start

commit v6 on v5

--- a/solution.py
+++ b/solution.py
@@ -10,7 +10,7 @@
 LANES = 128
 SIDE = 4
 GROUP = 8
-CHUNKS = ((0, 4), (8, 8), (24, 8), (16, 8), (4, 4))
+CHUNKS = ((0, 2), (2, 6), (8, 8), (16, 8), (24, 4), (28, 4))
 MESH = pl.DeviceIdType.MESH
 
 
@@ -19,9 +19,9 @@
 
 
 def moe_kernel(
-    tok_ref, grad_ref, ids_ref, wts_ref, gate_ref, up_ref, down_ref,
+    tok_ref, grad_ref, ids_ref, wts_ref, gate_hbm, up_hbm, down_hbm,
     mixed_out, tgrad_out, route_out, gate_out, up_out, down_out, back_ref, whole_ref,
-    square, tab_s, mine, blk, x_s, xt_s, g_s, hid_t, part, own, in_half, in_full, terms, rows_out, stage_a, stage_b,
+    gate_ref, up_ref, down_ref, square, tab_s, mine, blk, x_s, xt_s, g_s, hid_t, part, own, in_half, in_full, terms, rows_out, stage_a, stage_b,
     bk, mixed_acc, tgrad_acc, route_acc, final_v, route_in,
     ring_send, ring_recv, ret_send, ret_recv, a2a_send, a2a_recv, ag_send, ag_recv,
     pair_send, pair_recv, local_sem, stage_sem, fin_send, fin_recv,
@@ -45,6 +45,13 @@
     barrier = pltpu.get_barrier_semaphore()
     for m in range(1, n_dp):
         pl.semaphore_signal(barrier, inc=1, device_id={"dp": (d + m) % n_dp}, device_id_type=MESH)
+
+    loads = [
+        pltpu.make_async_copy(source, target, local_sem.at[7 + i])
+        for i, (source, target) in enumerate(((gate_hbm, gate_ref), (up_hbm, up_ref), (down_hbm, down_ref)))
+    ]
+    for item in loads:
+        item.start()
 
     def greet(step, carry):
         pl.semaphore_signal(
@@ -116,7 +123,7 @@
         )
 
     def spot(da, db, rel):
-        return db * GROUP + rel * SIDE + da
+        return db * GROUP + da * 2 + rel
 
     def ag_copy_to(axis, way, da, db, h):
         step = SIDE - 1 if way == 0 else 1
@@ -165,10 +172,12 @@
     def mine_copy():
         return pltpu.make_async_copy(block(0), mine, local_sem.at[5])
 
+    def own_phase():
+        launch(pair_copy(0, 0))
+        spread(0, 0, 0)
+        mine_copy().start()
+
     def first_phase():
-        spread(0, 0, 0)
-        launch(pair_copy(0, 0))
-        mine_copy().start()
         ag_wait(1, 0, 0)
         launch(ag_copy_to(0, 0, 1, 0, 0))
         ag_wait(3, 0, 1)
@@ -217,8 +226,8 @@
     def take_chunk(k):
         first, count = CHUNKS[k]
         for p in range(first, first + count):
-            if (p // SIDE) % 2 == 1:
-                pair_copy(p % SIDE, p // GROUP).wait_recv()
+            if p % 2 == 1:
+                pair_copy((p // 2) % SIDE, p // GROUP).wait_recv()
         load = pltpu.make_async_copy(
             whole_ref.at[pl.ds(first * toks, count * toks), :], blk.at[pl.ds(0, count * toks), :], local_sem.at[3]
         )
@@ -352,8 +361,8 @@
     def back_copy(k, i):
         db = CHUNKS[k][0] // GROUP
         p = CHUNKS[k][0] + i
-        s = (c + p // SIDE) % 2
-        da = p % SIDE
+        s = (c + p) % 2
+        da = (p // 2) % SIDE
         y2 = (y + da * (1 - s) + db * s) % SIDE
         z2 = (z + db * (1 - s) + da * s) % SIDE
         return pltpu.make_async_remote_copy(
@@ -382,7 +391,7 @@
         half = size_of(k) // 2
 
         def one(h, carry):
-            span = pl.ds(pl.multiple_of(CHUNKS[k][0] * slots_dp + h * half, half), half)
+            span = pl.ds(pl.multiple_of(CHUNKS[k][0] * slots_dp + h * half, slots_dp), half)
             rows_out[span, :width] = jnp.dot(
                 terms[0, span, :], down_ref[...], preferred_element_type=F32
             ).astype(BF)
@@ -411,8 +420,8 @@
         local = (row - index * slots_dp).astype(F32)
         p = first + index
         db = first // GROUP
-        da = p & (SIDE - 1)
-        core = (c + lax.shift_right_logical(p, 2)) & 1
+        da = lax.shift_right_logical(p, 1) & (SIDE - 1)
+        core = (c + p) & 1
         y2 = (y + 2 * SIDE - (da * (1 - c) + db * c)) & (SIDE - 1)
         z2 = (z + 2 * SIDE - (db * (1 - c) + da * c)) & (SIDE - 1)
         sender = (y2 * SIDE + z2) * 2 + core
@@ -525,36 +534,38 @@
         route_out[...] = result
 
     slices()
-    first_phase()
+    own_phase()
     last = len(CHUNKS)
+    for item in loads:
+        item.wait()
     take_chunk(0)
     stage0(0)
-    second_phase(0)
-    second_phase(1)
+    first_phase()
     for k in range(last + 1):
         if k < last:
             stage1(k)
         if k >= 1:
             stage3(k - 1)
-        if k == 0:
-            second_phase(3)
-            second_phase(2)
-            stage2(0)
         if k + 1 < last:
             take_chunk(k + 1)
             stage0(k + 1)
+        if k == 0:
+            second_phase(0)
+            second_phase(1)
+            stage2(0)
+            second_phase(3)
+            second_phase(2)
         if 1 <= k < last:
             stage2(k)
         if k == 1:
             for da in (0, 1, 3, 2):
                 third_phase(da)
-        if k == last:
-            fold(last - 3)
         if k >= 1:
             stage4(k - 1)
         if 2 <= k <= last - 2:
             fold(k - 2)
     weight_grads()
+    fold(last - 3)
     fold(last - 2)
     fold(last - 1)
     finish()
@@ -600,9 +611,12 @@
             jax.ShapeDtypeStruct((rows, both), BF),
             jax.ShapeDtypeStruct((experts * toks, both + LANES), BF),
         ),
-        in_specs=[inside] * 7,
+        in_specs=[anywhere, anywhere, inside, inside, anywhere, anywhere, anywhere],
         out_specs=(anywhere, anywhere, inside) + (anywhere,) * 5,
         scratch_shapes=[
+            vmem((width, hidden), BF),
+            vmem((width, hidden), BF),
+            vmem((hidden, width), BF),
             vmem((LANES, LANES), F32),
             vmem((tok_rows, LANES), BF),
             vmem((toks, both + LANES), BF),
@@ -635,7 +649,7 @@
             dma((SIDE * SIDE, 2)),
             dma((SIDE * SIDE,)),
             dma((SIDE * SIDE,)),
-            dma((7,)),
+            dma((10,)),
             dma((3, 2)),
             dma((n_dp, 3)),
             dma((n_dp - 1, 3)),

time: 248 us -> 242 us (0.976)
  Pallas kernels: 233 us -> 227 us
    pallas_call x1, Pallas kernels: 233 us -> 227 us  [moe(): pl.pallas_call(moe_kernel, out_shape=(jax.ShapeDtypeStruct(tokens.shape,...]
where the time goes in v6:
time: 242 us; the launch traced here: 239 us
  Pallas kernels  227 us (94%)
  local copies, waits for them, and re-layouts  10.9 us (5%)
    pallas_call x1, Pallas kernels, moe(): pl.pallas_call(moe_kernel, out_shape=(jax.ShapeDtypeStruct(tokens.shape,...  227 us
    unnamed x10, local copies, waits for them, and re-layouts  10.9 us

profile of v6, /device:TPU:34, one launch (start us, length us, event | category | flops | bytes accessed | tf_op | source)
XLA Modules:
  0.0 238.7 jit_solution(14041755079733148625)
XLA Ops:
  0.6 227.1 %shard_map.118 = (bf16[32,3584]{1,0:T(8,128)(2,1)}, bf16[32,3584]{1,0:T(8,128)(2,1)}, f32[8,32]{1,0:T(8,128)}, bf16[896,1024]{1,0:T(8,128)(2,1)}, bf16[896,1024]...) custom-call(bf16[32,3584]{1,0:T(8,128)(2,1)} %tok_ref.1, ...), custom_call_target="tpu_custom_call" | custom-call | tf_op jit(solution)/shard_map/pallas_call | solution.py:602
  227.7 1.6 copy.19
  229.3 1.6 copy.20
  231.0 1.3 copy.21
  232.3 0.0 copy-start.1
  232.3 3.0 %copy.22 = bf16[1,896,1024]{2,1,0:T(8,128)(2,1)} copy(bf16[1,896,1024]{2,1,0:T(8,128)(2,1)} %bitcast.11) | data formatting | bytes 3670016
  235.3 0.0 copy-done.1
  235.3 0.0 copy-start
  235.3 1.2 copy.23
  236.5 0.9 copy-done
  237.4 1.2 copy.24
Async XLA Ops:
  232.3 3.0 %copy-start.1 = (bf16[896,1024]{1,0:T(8,128)(2,1)S(1)}, bf16[896,1024]{1,0:T(8,128)(2,1)}, u32[]{:S(2)}) copy-start(bf16[896,1024]{1,0:T(8,128)(2,1)} %get-tuple-element.16) | copy-start | bytes 5505028
  235.3 2.2 copy-start

commit v7 on v6

--- a/solution.py
+++ b/solution.py
@@ -10,7 +10,7 @@
 LANES = 128
 SIDE = 4
 GROUP = 8
-CHUNKS = ((0, 2), (2, 6), (8, 8), (16, 8), (24, 4), (28, 4))
+CHUNKS = ((0, 2), (2, 2), (8, 8), (16, 8), (24, 4), (28, 4), (4, 4))
 MESH = pl.DeviceIdType.MESH
 
 
@@ -53,13 +53,12 @@
     for item in loads:
         item.start()
 
-    def greet(step, carry):
-        pl.semaphore_signal(
-            barrier, inc=1, device_id={"expert": (e + step) % experts}, device_id_type=MESH
-        )
-        return carry
-
-    lax.fori_loop(1, experts, greet, 0)
+    near = [e + 1 - 2 * c]
+    for step in (1, SIDE - 1):
+        near.append((((y + step) % SIDE) * SIDE + z) * 2 + c)
+        near.append((y * SIDE + (z + step) % SIDE) * 2 + c)
+    for peer in near:
+        pl.semaphore_signal(barrier, inc=1, device_id={"expert": peer}, device_id_type=MESH)
 
     def make_table():
         line = lax.broadcasted_iota(jnp.int32, (LANES, tok_rows), 0)
@@ -85,7 +84,7 @@
         tab_s[...] = square[...].T[:tok_rows].astype(BF)
 
     make_table()
-    pl.semaphore_wait(barrier, experts + n_dp - 2)
+    pl.semaphore_wait(barrier, len(near) + n_dp - 1)
 
     sends = []
 
@@ -560,9 +559,11 @@
         if k == 1:
             for da in (0, 1, 3, 2):
                 third_phase(da)
+        if k == last:
+            fold(last - 4)
         if k >= 1:
             stage4(k - 1)
-        if 2 <= k <= last - 2:
+        if 2 <= k <= last - 3:
             fold(k - 2)
     weight_grads()
     fold(last - 3)

time: 242 us -> 242 us (level)
  no operation moved by 1% of the time
where the time goes in v7:
time: 242 us; the launch traced here: 240 us
  Pallas kernels  228 us (94%)
  local copies, waits for them, and re-layouts  10.9 us (5%)
    pallas_call x1, Pallas kernels, moe(): pl.pallas_call(moe_kernel, out_shape=(jax.ShapeDtypeStruct(tokens.shape,...  228 us
    unnamed x10, local copies, waits for them, and re-layouts  10.9 us

profile of v7, /device:TPU:34, one launch (start us, length us, event | category | flops | bytes accessed | tf_op | source)
XLA Modules:
  0.0 239.6 jit_solution(14777155050744445495)
XLA Ops:
  0.6 228.0 %shard_map.118 = (bf16[32,3584]{1,0:T(8,128)(2,1)}, bf16[32,3584]{1,0:T(8,128)(2,1)}, f32[8,32]{1,0:T(8,128)}, bf16[896,1024]{1,0:T(8,128)(2,1)}, bf16[896,1024]...) custom-call(bf16[32,3584]{1,0:T(8,128)(2,1)} %tok_ref.1, ...), custom_call_target="tpu_custom_call" | custom-call | tf_op jit(solution)/shard_map/pallas_call | solution.py:603
  228.7 1.6 copy.19
  230.3 1.6 copy.20
  231.9 1.3 copy.21
  233.2 0.0 copy-start.1
  233.2 3.0 %copy.22 = bf16[1,896,1024]{2,1,0:T(8,128)(2,1)} copy(bf16[1,896,1024]{2,1,0:T(8,128)(2,1)} %bitcast.11) | data formatting | bytes 3670016
  236.2 0.0 copy-done.1
  236.2 0.0 copy-start
  236.2 1.2 copy.23
  237.5 0.9 copy-done
  238.4 1.2 copy.24
Async XLA Ops:
  233.2 3.0 %copy-start.1 = (bf16[896,1024]{1,0:T(8,128)(2,1)S(1)}, bf16[896,1024]{1,0:T(8,128)(2,1)}, u32[]{:S(2)}) copy-start(bf16[896,1024]{1,0:T(8,128)(2,1)} %get-tuple-element.16) | copy-start | bytes 5505028
  236.2 2.2 copy-start

commit v8 on v7

--- a/solution.py
+++ b/solution.py
@@ -10,7 +10,7 @@
 LANES = 128
 SIDE = 4
 GROUP = 8
-CHUNKS = ((0, 2), (2, 2), (8, 8), (16, 8), (24, 4), (28, 4), (4, 4))
+CHUNKS = ((0, 2), (2, 4), (8, 8), (16, 8), (24, 4), (28, 4), (6, 2))
 MESH = pl.DeviceIdType.MESH
 
 
@@ -541,10 +541,12 @@
     stage0(0)
     first_phase()
     for k in range(last + 1):
-        if k < last:
+        if k < last and k != 1:
             stage1(k)
-        if k >= 1:
+        if k > 1:
             stage3(k - 1)
+        if k == 1:
+            stage2(1)
         if k + 1 < last:
             take_chunk(k + 1)
             stage0(k + 1)
@@ -552,9 +554,11 @@
             second_phase(0)
             second_phase(1)
             stage2(0)
+            stage1(1)
             second_phase(3)
+            stage3(0)
             second_phase(2)
-        if 1 <= k < last:
+        if 2 <= k < last:
             stage2(k)
         if k == 1:
             for da in (0, 1, 3, 2):

time: 242 us -> 235 us (0.971)
  Pallas kernels: 228 us -> 220 us
    pallas_call x1, Pallas kernels: 228 us -> 220 us  [moe(): pl.pallas_call(moe_kernel, out_shape=(jax.ShapeDtypeStruct(tokens.shape,...]
where the time goes in v8:
time: 235 us; the launch traced here: 231 us
  Pallas kernels  220 us (94%)
  local copies, waits for them, and re-layouts  10.9 us (5%)
    pallas_call x1, Pallas kernels, moe(): pl.pallas_call(moe_kernel, out_shape=(jax.ShapeDtypeStruct(tokens.shape,...  220 us
    unnamed x10, local copies, waits for them, and re-layouts  10.9 us

profile of v8, /device:TPU:34, one launch (start us, length us, event | category | flops | bytes accessed | tf_op | source)
XLA Modules:
  0.0 231.4 jit_solution(16585902454198442996)
XLA Ops:
  0.6 219.8 %shard_map.118 = (bf16[32,3584]{1,0:T(8,128)(2,1)}, bf16[32,3584]{1,0:T(8,128)(2,1)}, f32[8,32]{1,0:T(8,128)}, bf16[896,1024]{1,0:T(8,128)(2,1)}, bf16[896,1024]...) custom-call(bf16[32,3584]{1,0:T(8,128)(2,1)} %tok_ref.1, ...), custom_call_target="tpu_custom_call" | custom-call | tf_op jit(solution)/shard_map/pallas_call | solution.py:607
  220.5 1.6 copy.19
  222.1 1.6 copy.20
  223.8 1.3 copy.21
  225.0 0.0 copy-start.1
  225.0 3.0 %copy.22 = bf16[1,896,1024]{2,1,0:T(8,128)(2,1)} copy(bf16[1,896,1024]{2,1,0:T(8,128)(2,1)} %bitcast.11) | data formatting | bytes 3670016
  228.0 0.0 copy-done.1
  228.0 0.0 copy-start
  228.0 1.2 copy.23
  229.3 0.9 copy-done
  230.2 1.2 copy.24
Async XLA Ops:
  225.0 3.0 %copy-start.1 = (bf16[896,1024]{1,0:T(8,128)(2,1)S(1)}, bf16[896,1024]{1,0:T(8,128)(2,1)}, u32[]{:S(2)}) copy-start(bf16[896,1024]{1,0:T(8,128)(2,1)} %get-tuple-element.16) | copy-start | bytes 5505028
  228.0 2.2 copy-start
